TPU v7x, 256 devices: a whole 4x4x8 slice. The times are simulated.
256 devices in a mesh: dp: 32 (over z, x), mp: 8 (over y, core).
Axes of the slice: x: 4, y: 4, z: 8, core: 2. Of those that a mesh axis runs over, the one named last changes fastest.
Arguments:
- input_steps: bfloat16 [4, 3072, 8192], P(None, 'dp', 'mp'), may hold values from -6 to 6
- gate_steps: bfloat16 [4, 3072, 8192], P(None, 'dp', 'mp'), may hold values from -6 to 6
- conv_state: bfloat16 [3072, 3, 8192], P('dp', None, 'mp'), may hold values from -6 to 6
- ssm_state: bfloat16 [3072, 16, 8192], P('dp', None, 'mp'), may hold values from -6 to 6
- new_slot: int32 [3072], replicated, may hold values from 0 to 3071, as said below
- remaining: int32 [3072], replicated, may hold values from 1 to 4
- conv_weight: float32 [4, 8192], P(None, 'mp'), may hold values from -3 to 3
- conv_bias: float32 [8192], P('mp'), may hold values from -3 to 3
- coef_proj: bfloat16 [8192, 544], P('mp', 'dp'), may hold values from -0.0625 to 0.0625
- delta_proj: bfloat16 [512, 8192], P('dp', 'mp'), may hold values from -0.25 to 0.25
- delta_bias: float32 [8192], P('mp'), may hold values from -4 to -1
- decay_log: float32 [16, 8192], P(None, 'mp'), may hold values from -1 to 2
- skip_gain: float32 [8192], P('mp'), may hold values from 0.5 to 1.5
- out_proj: bfloat16 [8192, 4096], P('mp', 'dp'), may hold values from -0.0625 to 0.0625
Outputs:
- layer_out: bfloat16 [4, 3072, 4096], P(None, 'dp', 'mp')
- conv_final: bfloat16 [3072, 3, 8192], P('dp', None, 'mp')
- ssm_final: bfloat16 [3072, 16, 8192], P('dp', None, 'mp')
Inputs may be any that keep to these rules, and one draw needn't show every extreme that they name: new_slot is a permutation of the rollouts. Each group hands to every group 0, 3 or 6 of its rollouts: 6 to exactly one group and 0 to exactly one group; each group receives 6 from exactly one group and 0 from exactly one group.
All inputs are finite; a program needn't handle non-finite values.
Results may differ from a plain program's by a relative error of at most 0.03.
Values may be sent and summed in bfloat16 or wider, within the bound.
No kernel may reach another device: no remote copies, remote signals or barrier semaphores. Data moves between devices by JAX's collectives and lax.ppermute only.
A program may use at most 128 MiB of HBM per device.

v0:
```python
import jax
import jax.numpy as jnp
from jax import lax
from jax.sharding import PartitionSpec as P


def per_device(
    input_steps,
    gate_steps,
    conv_state,
    ssm_state,
    new_slot,
    remaining,
    conv_weight,
    conv_bias,
    coef_proj,
    delta_proj,
    delta_bias,
    decay_log,
    skip_gain,
    out_proj,
):
    groups = lax.axis_size("dp")
    my_group = lax.axis_index("dp")
    row_count = conv_state.shape[0]
    channels = conv_state.shape[2]
    state_len = ssm_state.shape[1]
    steps_total = input_steps.shape[0]
    capacity = 2 * row_count // groups
    total_rows = new_slot.shape[0]
    target = new_slot // row_count
    group_ids = jnp.arange(groups, dtype=jnp.int32)
    marks = (target[:, None] == group_ids[None, :]).astype(jnp.int32)
    ranks = (
        jnp.cumsum(marks.reshape(groups, row_count, groups), axis=1).reshape(total_rows, groups) - 1
    )
    placed = jnp.sum(ranks * marks, axis=1)
    source = jnp.arange(total_rows, dtype=jnp.int32) // row_count
    inverse = (
        jnp.zeros((total_rows,), jnp.int32)
        .at[new_slot]
        .set(jnp.arange(total_rows, dtype=jnp.int32))
    )
    anchor = lax.dynamic_slice_in_dim(inverse, my_group * row_count, row_count)
    remain_new = remaining[anchor]
    my_target = lax.dynamic_slice_in_dim(target, my_group * row_count, row_count)
    my_placed = lax.dynamic_slice_in_dim(placed, my_group * row_count, row_count)
    from_group = source[anchor]
    from_rank = placed[anchor]

    def relocate(state):
        depth = state.shape[1]
        send_index = my_target * capacity + my_placed
        buffer = (
            jnp.zeros((groups * capacity, depth, channels), state.dtype).at[send_index].set(state)
        )
        moved = lax.all_to_all(buffer, "dp", split_axis=0, concat_axis=0, tiled=True)
        return moved[from_group * capacity + from_rank]

    coef_whole = lax.all_gather(coef_proj, "dp", axis=1, tiled=True)
    delta_whole = lax.all_gather(delta_proj, "dp", axis=0, tiled=True)
    rank_len = delta_whole.shape[0]
    decay_rate = -jnp.exp(decay_log)
    outputs = []
    window = relocate(conv_state).astype(jnp.float32)
    hidden = relocate(ssm_state).astype(jnp.float32)
    for position in range(steps_total):
        active = (remain_new > position)[:, None]
        full_window = jnp.concatenate(
            [window, input_steps[position].astype(jnp.float32)[:, None, :]], axis=1
        )
        conv_out = jnp.sum(full_window * conv_weight[None], axis=1) + conv_bias
        full_window, activated = (full_window, jax.nn.silu(conv_out))
        partial_value = jnp.dot(
            activated.astype(jnp.bfloat16), coef_whole, preferred_element_type=jnp.float32
        )
        low_rank = lax.psum(partial_value.astype(jnp.bfloat16), "mp").astype(jnp.float32)
        step_in = low_rank[:, :rank_len].astype(jnp.bfloat16)
        input_coef = low_rank[:, rank_len : rank_len + state_len]
        output_coef = low_rank[:, rank_len + state_len :]
        step_size = jax.nn.softplus(
            jnp.dot(step_in, delta_whole, preferred_element_type=jnp.float32) + delta_bias
        )
        step_size, input_coef, output_coef = (step_size, input_coef, output_coef)
        decay_factor = jnp.exp(step_size[:, None, :] * decay_rate[None])
        updated = (
            decay_factor * hidden + (step_size * activated)[:, None, :] * input_coef[:, :, None]
        )
        mixer = (
            jnp.sum(updated * output_coef[:, :, None], axis=1) + skip_gain * activated
        ) * jax.nn.silu(gate_steps[position].astype(jnp.float32))
        hidden = jnp.where(active[:, :, None], updated, hidden)
        window = jnp.where(active[:, :, None], full_window[:, 1:], window)
        outputs.append(jnp.where(active, mixer, 0.0).astype(jnp.bfloat16))
    stacked = jnp.stack(outputs).reshape(steps_total * row_count, channels)
    partial_mix = jnp.dot(
        stacked,
        lax.all_gather(out_proj, "dp", axis=1, tiled=True),
        preferred_element_type=jnp.float32,
    )
    summed = lax.psum_scatter(
        partial_mix.astype(jnp.bfloat16), "mp", scatter_dimension=1, tiled=True
    )
    layer_out = summed.reshape(steps_total, row_count, summed.shape[1])
    return (layer_out, window.astype(jnp.bfloat16), hidden.astype(jnp.bfloat16))


def solution(mesh):
    return jax.shard_map(
        per_device,
        mesh=mesh,
        in_specs=(
            P(None, "dp", "mp"),
            P(None, "dp", "mp"),
            P("dp", None, "mp"),
            P("dp", None, "mp"),
            P(),
            P(),
            P(None, "mp"),
            P("mp"),
            P("mp", "dp"),
            P("dp", "mp"),
            P("mp"),
            P(None, "mp"),
            P("mp"),
            P("mp", "dp"),
        ),
        out_specs=(P(None, "dp", "mp"), P("dp", None, "mp"), P("dp", None, "mp")),
        check_vma=False,
    )
```

profile of v0, /device:TPU:40, one launch (start us, length us, event | category | flops | bytes accessed | tf_op | source)
XLA Modules:
  0.0 467.4 jit_solution(12851053160211001335)
XLA Ops:
  7.2 0.8 compare_select_fusion.4
  8.0 0.1 eq.17
  8.1 0.1 copy.31
  8.2 2.5 select_reduce_fusion
  10.7 0.1 copy.32
  10.7 0.1 reduce_sum.100
  10.8 1.6 copy.33
  12.4 11.8 %scatter_custom_fusion = s32[3072]{0:T(1024)S(1)} fusion(s32[3072]{0:T(1024)S(1)} %get-tuple-element.40, s32[3072]{0:T(1024)S(1)} %iota.17, s32[]{:T(128)} %constant.48.clone.1), kind=kCustom, calls=%fused_computation.142 | custom fusion | bytes 12292 | tf_op jit(solution)/shard_map/scatter | solution.py:42
  24.2 0.1 compare_select_fusion.6
  24.3 1.5 broadcast_in_dim.143
  25.9 11.7 %scatter_fusion = bf16[192,3,1024]{2,1,0:T(4,128)(2,1)} fusion(bf16[192,3,1024]{2,1,0:T(4,128)(2,1)} %broadcast_in_dim.143, s32[96]{0:T(128)S(1)} %get-tuple-element.55, bf16[96,3,1024]{2,1,0:T(4,128)(2,1)S(1)} %copy.33), kind=kCustom, calls=%fused_computation.6 | custom fusion | bytes 1769856 | tf_op jit(solution)/shard_map/scatter | solution.py:55
  37.6 11.2 %all-to-all-start = ((bf16[192,3,1024]{2,1,0:T(4,128)(2,1)}), bf16[192,3,1024]{2,1,0:T(4,128)(2,1)}, u32[]{:S(2)}, u32[]{:S(2)}) async-start(bf16[192,3,1024]{2,1,0:T(4,128)(2,1)} %scatter_fusion), calls=%async_computation | async-start | bytes 3145728 | tf_op jit(solution)/shard_map/all_to_all | solution.py:57
  48.9 0.7 all-gather.9.cloned.1.call-update
  49.5 0.2 all-reduce.3.cloned.1.call-start
  49.8 1.1 gather_fusion.2
  51.0 1.1 gather_fusion.1
  52.1 1.1 gather_fusion
  53.3 0.5 broadcast_compare_fusion
  53.8 0.1 fusion.74
  53.9 0.6 fusion.45
  54.5 0.6 fusion.43
  55.1 75.8 %all-gather.9.cloned.1.call-done = bf16[32,17,1024]{2,1,0:T(8,128)(2,1)} async-done(((bf16[1,17,1024]{2,1,0:T(8,128)(2,1)}), bf16[32,17,1024]{2,1,0:T(8,128)(2,1)}) %all-gather.9.cloned.1.call-update) | async-done | bytes 1114128 | tf_op jit(solution)/shard_map/all_gather | solution.py:60
  130.9 2.4 reshape.544
  133.3 2.6 gather_fusion.3
  135.9 0.4 convert_element_type.144
  136.4 0.9 fusion.19
  137.3 0.9 fusion.15
  138.2 0.9 fusion.11
  139.1 6.2 %fusion.17 = (f32[96,1024]{1,0:T(8,128)S(1)}, f32[96,1024]{1,0:T(8,128)S(1)}, f32[96,1024]{1,0:T(8,128)S(1)}, f32[96,1024]{1,0:T(8,128)S(1)}) fusion(f32[96,1,1024]{2,1,0:T(1,128)S(1)} %get-tuple-element.54, f32[96,3,1024]{2,1,0:T(4,128)S(1)} %convert_element_type.144, f32[4,1024]{1,0:T(4,128)S(1)} %copy-done.15, f32[96,1,1024]{2,1,0:T(1,128)S(1)} %get-tuple-element.53, ...), kind=kLoop, calls=%fused_computation.44 | loop fusion | flops 4325376 | bytes 7880704 | tf_op jit(solution)/shard_map/reduce_sum | solution.py:72
  145.4 1.2 convolution_convert_fusion.1
  146.6 1.2 convolution_convert_fusion.2
  147.8 1.2 convolution_convert_fusion.3
  149.0 1.2 convolution_convert_fusion.4
  150.2 0.0 all-gather.5.cloned.1.call-start
  150.2 0.7 all-gather.5.cloned.1.call-update
  150.9 0.3 all-gather.7.cloned.1.call-start
  151.2 0.3 all-gather.7.cloned.1.call-update
  151.5 3.4 broadcast_in_dim.145
  154.9 14.7 %scatter_fusion.1 = bf16[192,16,1024]{2,1,0:T(8,128)(2,1)} fusion(bf16[192,16,1024]{2,1,0:T(8,128)(2,1)} %broadcast_in_dim.145, s32[96]{0:T(128)S(1)} %copy-done.18, bf16[96,16,1024]{2,1,0:T(8,128)(2,1)} %param.17), kind=kCustom, calls=%fused_computation.7 | custom fusion | bytes 9437568 | tf_op jit(solution)/shard_map/scatter | solution.py:55
  169.5 7.2 %all-to-all-start.1 = ((bf16[192,16,1024]{2,1,0:T(8,128)(2,1)}), bf16[192,16,1024]{2,1,0:T(8,128)(2,1)}, u32[]{:S(2)}, u32[]{:S(2)}) async-start(bf16[192,16,1024]{2,1,0:T(8,128)(2,1)} %scatter_fusion.1), calls=%async_computation.1 | async-start | bytes 12582912 | tf_op jit(solution)/shard_map/all_to_all | solution.py:57
  176.7 0.0 reduce-scatter.2.cloned.1.call-start
  176.8 1.6 exponential_negate_fusion
  178.3 34.8 %all-reduce.3.cloned.1.call-done = (bf16[96,544]{1,0:T(8,128)(2,1)}, bf16[96,544]{1,0:T(8,128)(2,1)}, bf16[96,544]{1,0:T(8,128)(2,1)}, bf16[96,544]{1,0:T(8,128)(2,1)}) async-done(((bf16[96,544]{1,0:T(8,128)(2,1)}, bf16[96,544]{1,0:T(8,128)(2,1)}, bf16[96,544]{1,0:T(8,128)(2,1)}, bf16[96,544]{1,0:T(8,128)(2,1)}), (bf16[96,544]{1,0:T(8,128)(2,1)}, bf16[96,544]{1,0:T(8,128)(2,1)}, bf16[96,544]{1,0:T(8,128)(2,1)}, ...) | async-done | bytes 417808 | tf_op jit(solution)/shard_map/psum | solution.py:77
  213.1 1.5 fusion.75
  214.6 1.5 fusion.76
  216.1 1.5 fusion.77
  217.6 1.5 fusion.78
  219.1 91.2 %all-gather.5.cloned.1.call-done = bf16[512,1024]{1,0:T(8,128)(2,1)} async-done(((bf16[16,1024]{1,0:T(8,128)(2,1)}), bf16[512,1024]{1,0:T(8,128)(2,1)}) %all-gather.5.cloned.1.call-update) | async-done | bytes 1048592 | tf_op jit(solution)/shard_map/all_gather | solution.py:61
  310.3 1.7 compare_select_fusion.1
  312.0 1.8 compare_select_fusion.2
  313.8 1.8 compare_select_fusion.3
  315.6 0.8 copy-done.33
  316.4 3.0 fusion.62
  319.5 5.3 %gather_fusion.4 = bf16[96,16,1024]{2,1,0:T(8,128)(2,1)} fusion(bf16[192,16,1024]{2,1,0:T(8,128)(2,1)} %all-to-all-done.1, s32[1024]{0:T(1024)S(1)} %pad_clamp_fusion), kind=kCustom, calls=%fused_computation.4 | custom fusion | bytes 6291840 | tf_op jit(solution)/shard_map/gather | solution.py:58
  324.8 7.6 %multiply_reduce_fusion.3 = (f32[96,1024]{1,0:T(8,128)S(1)}, f32[96,1024]{1,0:T(8,128)S(1)}) fusion(bf16[96,16,1024]{2,1,0:T(8,128)(2,1)} %gather_fusion.4, f32[96,16]{1,0:T(8,128)} %get-tuple-element.34, f32[96,16]{1,0:T(8,128)} %get-tuple-element.35, f32[96,1024]{1,0:T(8,128)} %get-tuple-element.45, f32[16,1024]{1,0:T(8,128)} %exponential_negate_fusion, ...), kind=kLoop, calls=%fused_computation.20 | loop fusion | flops 21823488 | bytes 5595232 | tf_op jit(solution)/shard_map/reduce_sum | solution.py:90
  332.5 12.6 %multiply_reduce_fusion.1 = (f32[96,1024]{1,0:T(8,128)S(1)}, f32[96,1024]{1,0:T(8,128)S(1)}) fusion(f32[96,16]{1,0:T(8,128)} %get-tuple-element.39, f32[96,16]{1,0:T(8,128)} %get-tuple-element.38, f32[96,1024]{1,0:T(8,128)} %get-tuple-element.43, f32[96,1024]{1,0:T(8,128)} %copy-done.36, f32[16,1024]{1,0:T(8,128)} %exponential_negate_fusion, ...), kind=kLoop, calls=%fused_computation.14 | loop fusion | flops 37552128 | bytes 7180576 | tf_op jit(solution)/shard_map/reduce_sum | solution.py:90
  345.1 1.1 fusion.50
  346.2 0.1 pad_maximum_fusion.4
  346.3 73.8 %all-gather.7.cloned.1.call-done = bf16[1024,4096]{1,0:T(8,128)(2,1)} async-done(((bf16[1024,128]{1,0:T(8,128)(2,1)}), bf16[1024,4096]{1,0:T(8,128)(2,1)}) %all-gather.7.cloned.1.call-update) | async-done | bytes 8388624 | tf_op jit(solution)/shard_map/all_gather | solution.py:98
  420.1 8.2 %convolution_convert_fusion = bf16[384,4096]{1,0:T(8,128)(2,1)} fusion(bf16[384,1024]{1,0:T(8,128)(2,1)S(1)} %bitcast.87, bf16[1024,4096]{1,0:T(8,128)(2,1)} %all-gather.7.cloned.1.call-done), kind=kOutput, calls=%fused_computation.21 | convolution fusion | flops 3222798336 | bytes 12320768 | tf_op jit(solution)/shard_map/dot_general | solution.py:96
  428.5 1.0 fusion.7
  429.4 1.0 copy.38
  430.5 11.6 %select_convert_fusion = bf16[96,16,1024]{2,1,0:T(8,128)(2,1)} fusion(f32[96,16]{1,0:T(8,128)S(1)} %copy-done.13, f32[96,1024]{1,0:T(8,128)} %get-tuple-element.42, f32[96,1024]{1,0:T(8,128)} %get-tuple-element.50, f32[96,16]{1,0:T(8,128)S(1)} %copy-done.14, f32[96,1024]{1,0:T(8,128)} %get-tuple-element.43, f32[96,1024]{1,0:T(8,128)} %copy-done.36, ...), kind=kLoop, calls=%fused_computation.11 | loop fusion | flops 34603008 | bytes 9527680 | tf_op jit(solution)/shard_map/convert_element_type | solution.py:105
  442.1 18.7 %reduce-scatter.2.cloned.1.call-done = bf16[384,512]{1,0:T(8,128)(2,1)} async-done(((bf16[384,4096]{1,0:T(8,128)(2,1)}), bf16[384,512]{1,0:T(8,128)(2,1)}) %reduce-scatter.2.cloned.1.call-update) | async-done | bytes 393232 | tf_op jit(solution)/shard_map/reduce_scatter | solution.py:101
  (83 shorter events, 0.3 us)
Async XLA Ops:
  7.2 44.9 %copy-start = (s32[3072]{0:T(1024)S(1)}, s32[3072]{0:T(1024)}, u32[]{:S(2)}) copy-start(s32[3072]{0:T(1024)} %param.19) | copy-start | bytes 36868
  7.2 46.6 %copy-start.8 = (bf16[4,96,1024]{2,1,0:T(8,128)(2,1)S(1)}, bf16[4,96,1024]{2,1,0:T(8,128)(2,1)}, u32[]{:S(2)}) copy-start(bf16[4,96,1024]{2,1,0:T(8,128)(2,1)} %param.14) | copy-start | bytes 2359300
  24.3 30.8 %copy-start.17 = (s32[96]{0:T(128)}, s32[96]{0:T(128)S(1)}, u32[]{:S(2)}) copy-start(s32[96]{0:T(128)S(1)} %get-tuple-element.55) | copy-start | bytes 1156
  37.6 95.7 %all-to-all-start = ((bf16[192,3,1024]{2,1,0:T(4,128)(2,1)}), bf16[192,3,1024]{2,1,0:T(4,128)(2,1)}, u32[]{:S(2)}, u32[]{:S(2)}) async-start(bf16[192,3,1024]{2,1,0:T(4,128)(2,1)} %scatter_fusion), calls=%async_computation | async-start | bytes 3145728 | tf_op jit(solution)/shard_map/all_to_all | solution.py:57
  48.8 82.1 %all-gather.9.cloned.1.call-start = ((), (), s32[]{:S(2)}) async-start(), calls=%async_computation.6 | async-start | bytes 1622016 | tf_op jit(solution)/shard_map/all_gather | solution.py:60
  49.5 163.6 %all-reduce.3.cloned.1.call-start = ((), (), s32[]{:S(2)}) async-start(), calls=%async_computation.7 | async-start | bytes 983040 | tf_op jit(solution)/shard_map/psum | solution.py:77
  53.8 83.5 %copy-start.25 = (pred[96]{0:T(512)(128)(4,1)}, pred[96]{0:T(512)(128)(4,1)S(1)}, u32[]{:S(2)}) copy-start(pred[96]{0:T(512)(128)(4,1)S(1)} %get-tuple-element.49) | copy-start | bytes 292
  53.8 83.5 %copy-start.22 = (pred[96]{0:T(512)(128)(4,1)}, pred[96]{0:T(512)(128)(4,1)S(1)}, u32[]{:S(2)}) copy-start(pred[96]{0:T(512)(128)(4,1)S(1)} %get-tuple-element.48) | copy-start | bytes 292
  53.8 84.4 %copy-start.19 = (pred[96]{0:T(512)(128)(4,1)}, pred[96]{0:T(512)(128)(4,1)S(1)}, u32[]{:S(2)}) copy-start(pred[96]{0:T(512)(128)(4,1)S(1)} %get-tuple-element.47) | copy-start | bytes 292
  135.9 3.2 copy-start.15
  138.2 7.2 %copy-start.7 = (bf16[544,1024]{1,0:T(8,128)(2,1)S(1)}, bf16[544,1024]{1,0:T(8,128)(2,1)}, u32[]{:S(2)}) copy-start(bf16[544,1024]{1,0:T(8,128)(2,1)} %reshape.544) | copy-start | bytes 3342340
  138.2 7.2 %copy-start.28 = (f32[1024]{0:T(1024)S(1)}, f32[1024]{0:T(1024)}, u32[]{:S(2)}) copy-start(f32[1024]{0:T(1024)} %param.21) | copy-start | bytes 12292
  145.4 2.4 copy-start.1
  145.4 3.6 copy-start.3
  145.4 3.6 copy-start.5
  147.8 7.1 %copy-start.18 = (s32[96]{0:T(128)S(1)}, s32[96]{0:T(128)}, u32[]{:S(2)}) copy-start(s32[96]{0:T(128)} %copy-done.17) | copy-start | bytes 1156
  150.2 160.2 %all-gather.5.cloned.1.call-start = ((), (), s32[]{:S(2)}) async-start(), calls=%async_computation.3 | async-start | bytes 1081344 | tf_op jit(solution)/shard_map/all_gather | solution.py:61
  150.9 269.2 %all-gather.7.cloned.1.call-start = ((), (), s32[]{:S(2)}) async-start(), calls=%async_computation.4 | async-start | bytes 8650752 | tf_op jit(solution)/shard_map/all_gather | solution.py:98
  169.5 149.9 %all-to-all-start.1 = ((bf16[192,16,1024]{2,1,0:T(8,128)(2,1)}), bf16[192,16,1024]{2,1,0:T(8,128)(2,1)}, u32[]{:S(2)}, u32[]{:S(2)}) async-start(bf16[192,16,1024]{2,1,0:T(8,128)(2,1)} %scatter_fusion.1), calls=%async_computation.1 | async-start | bytes 12582912 | tf_op jit(solution)/shard_map/all_to_all | solution.py:57
  176.7 139.7 %copy-start.2 = (f32[96,1024]{1,0:T(8,128)S(1)}, f32[96,1024]{1,0:T(8,128)}, u32[]{:S(2)}) copy-start(f32[96,1024]{1,0:T(8,128)} %copy-done.1) | copy-start | bytes 1179652
  176.7 139.7 %copy-start.4 = (f32[96,1024]{1,0:T(8,128)S(1)}, f32[96,1024]{1,0:T(8,128)}, u32[]{:S(2)}) copy-start(f32[96,1024]{1,0:T(8,128)} %copy-done.3) | copy-start | bytes 1179652
  176.7 139.7 %copy-start.6 = (f32[96,1024]{1,0:T(8,128)S(1)}, f32[96,1024]{1,0:T(8,128)}, u32[]{:S(2)}) copy-start(f32[96,1024]{1,0:T(8,128)} %copy-done.5) | copy-start | bytes 1179652
  176.7 284.1 %reduce-scatter.2.cloned.1.call-start = ((), (), s32[]{:S(2)}) async-start(), calls=%async_computation.5 | async-start | bytes 3538944 | tf_op jit(solution)/shard_map/reduce_scatter | solution.py:101
  312.0 3.6 copy-start.36
  313.8 1.8 copy-start.31
  315.6 0.8 copy-start.33
  332.4 12.7 %copy-start.9 = (bf16[4,96,1024]{2,1,0:T(8,128)(2,1)S(1)}, bf16[4,96,1024]{2,1,0:T(8,128)(2,1)}, u32[]{:S(2)}) copy-start(bf16[4,96,1024]{2,1,0:T(8,128)(2,1)} %param.15) | copy-start | bytes 2359300
  332.4 12.7 %copy-start.16 = (pred[96]{0:T(512)(128)(4,1)S(1)}, pred[96]{0:T(512)(128)(4,1)}, u32[]{:S(2)}) copy-start(pred[96]{0:T(512)(128)(4,1)} %get-tuple-element.46) | copy-start | bytes 292
  332.4 12.7 %copy-start.20 = (pred[96]{0:T(512)(128)(4,1)S(1)}, pred[96]{0:T(512)(128)(4,1)}, u32[]{:S(2)}) copy-start(pred[96]{0:T(512)(128)(4,1)} %copy-done.19) | copy-start | bytes 292
  332.4 12.7 %copy-start.23 = (pred[96]{0:T(512)(128)(4,1)S(1)}, pred[96]{0:T(512)(128)(4,1)}, u32[]{:S(2)}) copy-start(pred[96]{0:T(512)(128)(4,1)} %copy-done.22) | copy-start | bytes 292
  332.4 12.7 %copy-start.26 = (pred[96]{0:T(512)(128)(4,1)S(1)}, pred[96]{0:T(512)(128)(4,1)}, u32[]{:S(2)}) copy-start(pred[96]{0:T(512)(128)(4,1)} %copy-done.25) | copy-start | bytes 292
  332.4 12.7 %copy-start.29 = (f32[1024]{0:T(1024)S(1)}, f32[1024]{0:T(1024)}, u32[]{:S(2)}) copy-start(f32[1024]{0:T(1024)} %param.21) | copy-start | bytes 12292
  332.5 12.7 %copy-start.30 = (f32[1024]{0:T(1024)S(1)}, f32[1024]{0:T(1024)}, u32[]{:S(2)}) copy-start(f32[1024]{0:T(1024)} %param.26) | copy-start | bytes 12292
  428.3 2.1 copy-start.10
  428.3 2.1 copy-start.11
  428.4 2.1 copy-start.12
  428.4 2.1 copy-start.13
  428.4 2.1 copy-start.14
  428.4 2.1 copy-start.21
  428.4 2.1 copy-start.24
  428.4 2.1 copy-start.27
  428.4 2.1 copy-start.32
  428.4 2.1 copy-start.34
  428.4 2.1 copy-start.35
Sparse Core Ops, SparseCore 0:
  52.2 78.6 all-gather.8
  150.3 62.8 all-reduce.2
  216.1 94.2 all-gather.4
  312.9 107.1 all-gather.6
  428.6 32.2 reduce-scatter.1
where the time goes:
time: 473 us; the launch traced here: 467 us
  waiting for transfers between devices  296 us (63%)
  local copies, waits for them, and re-layouts  66.8 us (14%)
  other arithmetic  49.9 us (11%)
  matrix products  21.2 us (4%)
  starting transfers between devices  19 us (4%)
  between operations  14.4 us (3%)
    all_gather x1, waiting for transfers between devices, per_device(): delta_whole = lax.all_gather(delta_proj, 'dp', axis=0, tiled=True)  91.2 us
    all_gather x1, waiting for transfers between devices, per_device(): coef_whole = lax.all_gather(coef_proj, 'dp', axis=1, tiled=True)  75.8 us
    all_gather x1, waiting for transfers between devices, per_device(): lax.all_gather(out_proj, 'dp', axis=1, tiled=True)  73.8 us
    psum x1, waiting for transfers between devices, per_device(): lax.psum(partial_value.astype(jnp.bfloat16), 'mp').astype(jnp.float32)  34.8 us
    scatter x2, local copies, waits for them, and re-layouts, relocate(): jnp.zeros((groups * capacity, depth, channels), state.dtype).at[send_index]  26.3 us
    reduce_sum x2, other arithmetic, per_device(): jnp.sum(updated * output_coef[:, :, None], axis=1) + skip_gain * activated  20.1 us
    reduce_scatter x1, waiting for transfers between devices, per_device(): lax.psum_scatter(partial_mix.astype(jnp.bfloat16), 'mp', scatter_dimensio...  18.7 us
    all_to_all x2, starting transfers between devices, relocate(): lax.all_to_all(buffer, 'dp', split_axis=0, concat_axis=0, tiled=True)  18.4 us
  transfers between devices with their start and end apart: 7, of which 5 were waited for; matrix products, arithmetic and copies ran while one was open for 18% of the time, Pallas kernels for 0%

commit v1 on v0

v1 whole, which is shorter than its diff:
```python
import functools

import jax
import jax.numpy as jnp
from jax import lax
from jax.experimental import pallas as pl
from jax.experimental.pallas import tpu as pltpu
from jax.sharding import Mesh
from jax.sharding import PartitionSpec as P

BF = jnp.bfloat16
F32 = jnp.float32
I32 = jnp.int32
NZ, NX, NY, NC = 8, 4, 4, 2
GROUPS = NZ * NX
ROWS = 96
CH = 1024
STATE = 16
RANK = 512
STEPS = 4
LOW = RANK + 2 * STATE
COEF = LOW // GROUPS
DELTA = RANK // GROUPS
BASE = ROWS // GROUPS
SLOT = 16
SEC = 32
GATH = SEC + DELTA
LOG2E = 1.4426950408889634
VMEM = pl.BlockSpec(memory_space=pltpu.VMEM)
SMEM = pl.BlockSpec(memory_space=pltpu.SMEM)
ANY = pl.BlockSpec(memory_space=pl.ANY)


def iota(shape, dim):
    return lax.broadcasted_iota(I32, shape, dim)


def bdot(a, b):
    return jnp.dot(a, b, preferred_element_type=F32)


def bdot_t(a, b):
    return lax.dot_general(a, b, (((1,), (1,)), ((), ())), preferred_element_type=F32)


def onehot(cond):
    return cond.astype(F32).astype(BF)


def plan_kernel(
    me_ref, slots_ref, remaining_ref, mine_ref, conv_ref, coef_ref,
    pack_ref, gather_ref, rem_ref, col_ref, ext_ref, buf_ref, sec_ref,
):
    me = me_ref[0]
    match = (slots_ref[...] == me * ROWS + iota((ROWS, GROUPS * ROWS), 0)).astype(I32)
    inv = jnp.sum(match * iota(match.shape, 1), axis=1, keepdims=True)
    rem_ref[...] = jnp.sum(match * remaining_ref[...], axis=1, keepdims=True)
    square = (ROWS, ROWS)
    eye = iota(square, 0) == iota(square, 1)
    inv_row = jnp.sum(jnp.where(eye, inv, 0), axis=0, keepdims=True)
    src = inv // ROWS
    src_row = inv_row // ROWS
    rank = jnp.sum(
        ((src == src_row) & (inv_row < inv)).astype(I32), axis=1, keepdims=True
    )
    rank_row = jnp.sum(
        ((src == src_row) & (inv < inv_row)).astype(I32), axis=0, keepdims=True
    )
    base_row = src_row * BASE + rank_row
    where_row = jnp.where(rank_row < BASE, base_row, ROWS + base_row - BASE)
    gather_ref[...] = jnp.broadcast_to(where_row, gather_ref.shape)
    for tap in range(3):
        at = pl.ds(tap * ROWS, ROWS)
        col_ref[at, :] = jnp.where(rank < BASE, src * SLOT + rank * 3 + tap, -1)
        ext_ref[at, :] = jnp.where(
            rank < BASE, -1, src * GATH + COEF + (rank - BASE) * 3 + tap
        )
    to_row = mine_ref[...] // ROWS
    to = jnp.sum(jnp.where(eye, to_row, 0), axis=1, keepdims=True)
    same = to == to_row
    order_row = jnp.sum((same & (iota(square, 0) < iota(square, 1))).astype(I32), axis=0, keepdims=True)
    order = jnp.sum((same & (iota(square, 1) < iota(square, 0))).astype(I32), axis=1, keepdims=True)
    place = jnp.where(order < BASE, to * BASE + order, ROWS + order - BASE)
    lanes = (ROWS, 128)
    picked = jnp.sum(jnp.where(place == iota(lanes, 1), iota(lanes, 0), 0), axis=0, keepdims=True)
    pack_ref[...] = jnp.broadcast_to(picked, pack_ref.shape)
    buf = jnp.zeros((GROUPS * SLOT, CH), F32)
    sec = bdot(onehot(iota((SEC, COEF), 0) == iota((SEC, COEF), 1)), coef_ref[...])
    for tap in range(3):
        dest = jnp.where(order_row < BASE, to_row * SLOT + order_row * 3 + tap, -1)
        buf += bdot(onehot(iota((GROUPS * SLOT, ROWS), 0) == dest), conv_ref[tap])
        dest = jnp.where(order_row < BASE, -1, COEF + (order_row - BASE) * 3 + tap)
        sec += bdot(onehot(iota((SEC, ROWS), 0) == dest), conv_ref[tap])
    buf_ref[...] = buf.astype(BF)
    sec_ref[...] = sec.astype(BF)


def plan(me, slots, remaining, mine, conv, coef):
    shape = jax.ShapeDtypeStruct
    return pl.pallas_call(
        plan_kernel,
        name="plan",
        out_shape=(
            shape((8, 128), I32),
            shape((8, ROWS), I32),
            shape((ROWS, 1), I32),
            shape((3 * ROWS, 1), I32),
            shape((3 * ROWS, 1), I32),
            shape((GROUPS * SLOT, CH), BF),
            shape((SEC, CH), BF),
        ),
        in_specs=[SMEM] + [VMEM] * 5,
        out_specs=(VMEM,) * 7,
        compiler_params=pltpu.CompilerParams(vmem_limit_bytes=40 << 20),
    )(me, slots, remaining, mine, conv, coef)


def pack_kernel(pick_ref, ssm_ref, main_ref, extra_ref, sems):
    def send(p, carry):
        pltpu.make_async_copy(ssm_ref.at[pick_ref[0, p]], main_ref.at[p], sems.at[0]).start()
        return carry

    lax.fori_loop(0, ROWS, send, 0)
    for p in range(BASE):
        pltpu.make_async_copy(ssm_ref.at[pick_ref[0, ROWS + p]], extra_ref.at[p], sems.at[1]).start()
    pltpu.make_async_copy(ssm_ref, main_ref, sems.at[0]).wait()
    pltpu.make_async_copy(ssm_ref.at[pl.ds(0, BASE)], extra_ref, sems.at[1]).wait()


def pack(pick, ssm):
    shape = jax.ShapeDtypeStruct
    return pl.pallas_call(
        pack_kernel,
        name="pack",
        out_shape=(shape((ROWS, STATE, CH), BF), shape((BASE, STATE, CH), BF)),
        in_specs=[SMEM, ANY],
        out_specs=(ANY, ANY),
        scratch_shapes=[pltpu.SemaphoreType.DMA((2,))],
        compiler_params=pltpu.CompilerParams(vmem_limit_bytes=8 << 20),
    )(pick, ssm)


def conv_kernel(
    me_ref, moved_ref, g0, g1, g2, g3, col_ref, ext_ref, rem_ref, inputs_ref, weight_ref, bias_ref,
    act_ref, low_ref, final_ref,
):
    x = me_ref[1]
    parts = (g0, g1, g2, g3)
    span = NZ * GATH
    window = bdot(onehot(col_ref[...] == iota((3 * ROWS, GROUPS * SLOT), 1)), moved_ref[...])
    coef = jnp.zeros((LOW, CH), F32)
    for k, part in enumerate(parts):
        at = iota((1, span), 1)
        z, q = at // GATH, at % GATH
        group = z * NX + lax.rem(x - k + NX, NX)
        ext = onehot(ext_ref[...] == group * GATH + q)
        window += bdot(ext, part[...])
        row = jnp.where(q < COEF, group * COEF + q, -1)
        coef += bdot(onehot(iota((LOW, span), 0) == row), part[...])
    coef = coef.astype(BF)
    taps = [window[tap * ROWS : (tap + 1) * ROWS] for tap in range(3)]
    taps += [inputs_ref[t].astype(F32) for t in range(STEPS)]
    weight = weight_ref[...]
    for t in range(STEPS):
        out = bias_ref[...] + sum(taps[t + k] * weight[k : k + 1] for k in range(4))
        act = out / (1.0 + jnp.exp(-out))
        act_ref[t] = act
        low_ref[pl.ds(t * ROWS, ROWS), :] = bdot_t(act.astype(BF), coef).astype(BF)
    rem = rem_ref[...]
    for k in range(3):
        kept = taps[k]
        for t in range(1, STEPS + 1):
            kept = jnp.where(rem >= t, taps[t + k], kept)
        final_ref[k] = kept.astype(BF)


def conv_stage(me, moved, parts, col, ext, rem, inputs, weight, bias):
    shape = jax.ShapeDtypeStruct
    return pl.pallas_call(
        conv_kernel,
        name="conv",
        out_shape=(
            shape((STEPS, ROWS, CH), F32),
            shape((STEPS * ROWS, LOW), BF),
            shape((3, ROWS, CH), BF),
        ),
        in_specs=[SMEM] + [VMEM] * 11,
        out_specs=(VMEM,) * 3,
        compiler_params=pltpu.CompilerParams(vmem_limit_bytes=56 << 20),
    )(me, moved, *parts, col, ext, rem, inputs, weight, bias)


def step_kernel(
    me_ref, own_ref, other_ref, g0, g1, g2, g3, bias_ref, act_ref, gate_ref, skip_ref, rem_ref, log_ref,
    dt_ref, dx_ref, sk_ref, sg_ref, bc_ref, rate_ref, low_ref,
):
    x, y, c = me_ref[1], me_ref[2], me_ref[3]
    rate_ref[...] = -jnp.exp(log_ref[...]) * LOG2E
    chunk = STEPS * ROWS // (NY * NC)
    for half, piece in ((c, own_ref), (1 - c, other_ref)):
        for m in range(NY):
            at = half * NY + lax.rem(y + m, NY)
            low_ref[pl.ds(pl.multiple_of(at * chunk, 16), chunk), :] = piece[m]
    span = NZ * GATH
    delta = jnp.zeros((RANK, CH), F32)
    for k, part in enumerate((g0, g1, g2, g3)):
        at = iota((1, span), 1)
        z, q = at // GATH, at % GATH
        group = z * NX + lax.rem(x - k + NX, NX)
        row = jnp.where(q >= SEC, group * DELTA + q - SEC, -1)
        delta += bdot(onehot(iota((RANK, span), 0) == row), part[...])
    delta = delta.astype(BF)
    rem = rem_ref[...]
    for t in range(STEPS):
        low = low_ref[pl.ds(t * ROWS, ROWS), :]
        raw = bdot(low[:, :RANK], delta) + bias_ref[...]
        size = jnp.maximum(raw, 0.0) + jnp.log1p(jnp.exp(-jnp.abs(raw)))
        active = rem > t
        size = jnp.where(active, size, 0.0)
        act = act_ref[t]
        gate = gate_ref[t].astype(F32)
        dt_ref[t] = size
        dx_ref[t] = size * act
        sk_ref[t] = skip_ref[...] * act
        sg_ref[t] = jnp.where(active, gate / (1.0 + jnp.exp(-gate)), 0.0)
        coefs = low[:, RANK:].astype(F32)
        for n in range(2 * STATE):
            bc_ref[t, n] = jnp.broadcast_to(coefs[:, n : n + 1], (ROWS, 128))


def step_stage(me, own, other, parts, bias, act, gate, skip, rem, log):
    shape = jax.ShapeDtypeStruct
    rows = shape((STEPS, ROWS, CH), F32)
    return pl.pallas_call(
        step_kernel,
        name="sizes",
        out_shape=(rows, rows, rows, rows, shape((STEPS, 2 * STATE, ROWS, 128), F32), shape((STATE, CH), F32)),
        in_specs=[SMEM] + [VMEM] * 12,
        out_specs=(VMEM,) * 6,
        scratch_shapes=[pltpu.VMEM((STEPS * ROWS, LOW), BF)],
        compiler_params=pltpu.CompilerParams(vmem_limit_bytes=56 << 20),
    )(me, own, other, *parts, bias, act, gate, skip, rem, log)


BLOCK = 8
BLOCKS = ROWS // BLOCK


def scan_kernel(
    at_ref, main_ref, extra_ref, dt_ref, dx_ref, sk_ref, sg_ref, bc_ref, rate_ref,
    out_ref, final_ref, held, wide, sems,
):
    b = pl.program_id(0)

    def fetch(block):
        for i in range(BLOCK):
            at = at_ref[0, block * BLOCK + i]

            @pl.when(at < ROWS)
            def _():
                pltpu.make_async_copy(main_ref.at[at], held.at[block, i], sems.at[block]).start()

            @pl.when(at >= ROWS)
            def _():
                pltpu.make_async_copy(extra_ref.at[at - ROWS], held.at[block, i], sems.at[block]).start()

    @pl.when(b == 0)
    def _():
        for block in range(3):
            fetch(block)

    @pl.when(b + 3 < BLOCKS)
    def _():
        fetch(b + 3)

    pltpu.make_async_copy(main_ref.at[pl.ds(0, BLOCK)], held.at[b], sems.at[b]).wait()
    for i in range(BLOCK):
        for l in range(CH // 128):
            wide[l, pl.ds(i * STATE, STATE), :] = held[b, i, :, pl.ds(l * 128, 128)].astype(F32)

    def lanes(l, carry):
        cols = pl.ds(pl.multiple_of(l * 128, 128), 128)
        dts = [dt_ref[t, :, cols] for t in range(STEPS)]
        dxs = [dx_ref[t, :, cols] for t in range(STEPS)]
        sums = [sk_ref[t, :, cols] for t in range(STEPS)]
        for n in range(STATE):
            here = pl.ds(n, BLOCK, stride=STATE)
            h = wide[l, here, :]
            rate = jnp.broadcast_to(rate_ref[pl.ds(n, 1), cols], (BLOCK, 128))
            for t in range(STEPS):
                h = jnp.exp2(dts[t] * rate) * h + dxs[t] * bc_ref[t, n]
                sums[t] += h * bc_ref[t, STATE + n]
            wide[l, here, :] = h
        for t in range(STEPS):
            out_ref[t, :, cols] = (sums[t] * sg_ref[t, :, cols]).astype(BF)
        return carry

    lax.fori_loop(0, CH // 128, lanes, 0)
    for i in range(BLOCK):
        for l in range(CH // 128):
            final_ref[i, :, pl.ds(l * 128, 128)] = wide[l, pl.ds(i * STATE, STATE), :].astype(BF)


def scan_stage(at, main, extra, dt, dx, sk, sg, bc, rate):
    shape = jax.ShapeDtypeStruct
    rows = pl.BlockSpec((STEPS, BLOCK, CH), lambda b, at: (0, b, 0))
    return pl.pallas_call(
        scan_kernel,
        name="scan",
        out_shape=(shape((STEPS, ROWS, CH), BF), shape((ROWS, STATE, CH), BF)),
        grid_spec=pltpu.PrefetchScalarGridSpec(
            num_scalar_prefetch=1,
            grid=(BLOCKS,),
            in_specs=[
                ANY,
                ANY,
                rows,
                rows,
                rows,
                rows,
                pl.BlockSpec((STEPS, 2 * STATE, BLOCK, 128), lambda b, at: (0, 0, b, 0)),
                pl.BlockSpec((STATE, CH), lambda b, at: (0, 0)),
            ],
            out_specs=(rows, pl.BlockSpec((BLOCK, STATE, CH), lambda b, at: (b, 0, 0))),
            scratch_shapes=[
                pltpu.VMEM((BLOCKS, BLOCK, STATE, CH), BF),
                pltpu.VMEM((CH // 128, BLOCK * STATE, 128), F32),
                pltpu.SemaphoreType.DMA((BLOCKS,)),
            ],
        ),
        compiler_params=pltpu.CompilerParams(vmem_limit_bytes=40 << 20),
    )(at, main, extra, dt, dx, sk, sg, bc, rate)


def shift(value, axis, size, k):
    return lax.ppermute(value, axis, [(i, (i + k) % size) for i in range(size)])


def reduce_mp(low, y, c):
    chunk = STEPS * ROWS // (NY * NC)
    halves = low.reshape(NC, NY * chunk, LOW)
    got = shift(lax.dynamic_index_in_dim(halves, 1 - c, 0, False), "c", NC, 1)
    mine = lax.dynamic_index_in_dim(halves, c, 0, False).astype(F32) + got.astype(F32)
    quarters = mine.reshape(NY, chunk, LOW)
    rounded = quarters.astype(BF)
    total = lax.dynamic_index_in_dim(quarters, y, 0, False)
    came = [
        shift(lax.dynamic_index_in_dim(rounded, lax.rem(y + k, NY), 0, False), "y", NY, k)
        for k in range(1, NY)
    ]
    total = (total + came[0].astype(F32) + came[1].astype(F32) + came[2].astype(F32)).astype(BF)
    own = jnp.stack([total] + [shift(total, "y", NY, NY - m) for m in range(1, NY)])
    return own, shift(own, "c", NC, 1)


def per_device(
    input_steps, gate_steps, conv_state, ssm_state, new_slot, remaining, conv_weight, conv_bias,
    coef_proj, delta_proj, delta_bias, decay_log, skip_gain, out_proj,
):
    z, x, y, c = (lax.axis_index(name) for name in ("z", "x", "y", "c"))
    group = z * NX + x
    me = jnp.stack([group, x, y, c]).astype(I32)
    out_whole = lax.all_gather(out_proj, ("z", "x"), axis=1, tiled=True)
    mine = lax.dynamic_slice_in_dim(new_slot, group * ROWS, ROWS)
    pick, at, rem, col, ext, buf, sec = plan(
        me,
        new_slot.reshape(1, -1),
        remaining.reshape(1, -1),
        mine.reshape(1, -1),
        conv_state.transpose(1, 0, 2),
        coef_proj.T,
    )
    moved = lax.all_to_all(
        buf.reshape(GROUPS, SLOT, CH), ("z", "x"), split_axis=0, concat_axis=0, tiled=True
    ).reshape(GROUPS * SLOT, CH)
    main, extra = pack(pick, ssm_state)
    gathered = lax.all_gather(
        jnp.concatenate([sec, delta_proj], axis=0), "z", axis=0, tiled=True
    )
    parts = [gathered] + [shift(gathered, "x", NX, k) for k in range(1, NX)]
    ssm_main = lax.all_to_all(main, ("z", "x"), split_axis=0, concat_axis=0, tiled=True)
    extras = lax.all_gather(extra.reshape(BASE * STATE, CH), "z", axis=0, tiled=True)
    extras = extras.reshape(NZ, BASE, STATE, CH)
    extras = [extras] + [shift(extras, "x", NX, k) for k in range(1, NX)]
    act, low, conv_final = conv_stage(
        me, moved, parts, col, ext, rem, input_steps, conv_weight, conv_bias.reshape(1, -1)
    )
    own, other = reduce_mp(low, y, c)
    dt, dx, sk, sg, bc, rate = step_stage(
        me, own, other, parts, delta_bias.reshape(1, -1), act, gate_steps, skip_gain.reshape(1, -1), rem, decay_log
    )
    spot = at[:1] - ROWS
    their = spot // BASE
    turned = (lax.rem(x - their % NX + NX, NX) * NZ + their // NX) * BASE + spot % BASE
    at = jnp.where(at[:1] < ROWS, at[:1], ROWS + turned)
    stepped, ssm_final = scan_stage(
        at, ssm_main, jnp.concatenate(extras, axis=0).reshape(ROWS, STATE, CH), dt, dx, sk, sg, bc, rate
    )
    partial_mix = bdot(stepped.reshape(STEPS * ROWS, CH), out_whole)
    summed = lax.psum_scatter(partial_mix.astype(BF), ("y", "c"), scatter_dimension=1, tiled=True)
    return summed.reshape(STEPS, ROWS, -1), conv_final.transpose(1, 0, 2), ssm_final


def solution(mesh):
    fine = Mesh(mesh.devices.reshape(NZ, NX, NY, NC), ("z", "x", "y", "c"))
    dp, mp = ("z", "x"), ("y", "c")
    return jax.shard_map(
        per_device,
        mesh=fine,
        in_specs=(
            P(None, dp, mp),
            P(None, dp, mp),
            P(dp, None, mp),
            P(dp, None, mp),
            P(),
            P(),
            P(None, mp),
            P(mp),
            P(mp, dp),
            P(dp, mp),
            P(mp),
            P(None, mp),
            P(mp),
            P(mp, dp),
        ),
        out_specs=(P(None, dp, mp), P(dp, None, mp), P(dp, None, mp)),
        check_vma=False,
    )
```

time: 473 us -> 381 us (0.81)
  waiting for transfers between devices: 296 us -> 102 us
  blocking collectives: 0 us -> 143 us
  Pallas kernels: 0 us -> 48.1 us
  local copies, waits for them, and re-layouts: 66.8 us -> 19.4 us
  other arithmetic: 49.9 us -> 5.49 us
  starting transfers between devices: 19 us -> 35.8 us
  matrix products: 21.2 us -> 8.68 us
    all_gather x3 -> x1, waiting for transfers between devices: 241 us -> 0.01 us  [per_device(): out_whole = lax.all_gather(out_proj, ('z', 'x'), axis=1, tiled=True)]
    all_gather x0 -> x2, blocking collectives: none -> 143 us  [the longest x1 115 us: per_device(): lax.all_gather(jnp.concatenate([sec, delta_proj], axis=0), 'z', axis=0, t...]
    pallas_call x0 -> x5, Pallas kernels: none -> 48.1 us  [the longest x1 19.3 us: scan_stage(): pl.pallas_call(scan_kernel, name='scan', out_shape=(shape((STEPS, ROWS, C...]
    ppermute x0 -> x14, waiting for transfers between devices: none -> 44.1 us  [shift(): return lax.ppermute(value, axis, [(i, (i + k) % size) for i in range(size)])]
    scatter x3 -> x0, local copies, waits for them, and re-layouts: 38.1 us -> none  [the longest x2 26.3 us: relocate(): jnp.zeros((groups * capacity, depth, channels), state.dtype).at[send_index]]
    psum x1 -> x0, waiting for transfers between devices: 34.8 us -> none  [per_device(): lax.psum(partial_value.astype(jnp.bfloat16), 'mp').astype(jnp.float32)]
    reduce_sum x3 -> x0, other arithmetic: 26.4 us -> none  [the longest x2 20.1 us: per_device(): jnp.sum(updated * output_coef[:, :, None], axis=1) + skip_gain * activated]
    all_to_all x2, waiting for transfers between devices: 0.01 us -> 23.4 us  [the longest x1 23.4 us: per_device(): lax.all_to_all(buf.reshape(GROUPS, SLOT, CH), ('z', 'x'), split_axis=0, c...]
  transfers between devices with their start and end apart: 7 -> 18, of which waited for: 5 -> 12; matrix products, arithmetic and copies ran while one was open for 18% -> 2% of each run, Pallas kernels for 0% -> 13%
where the time goes in v1:
time: 381 us; the launch traced here: 377 us
  blocking collectives  143 us (38%)
  waiting for transfers between devices  102 us (27%)
  Pallas kernels  48.1 us (13%)
  starting transfers between devices  35.8 us (9%)
  local copies, waits for them, and re-layouts  19.4 us (5%)
  between operations  14.3 us (4%)
  matrix products  8.68 us (2%)
  other arithmetic  5.49 us (1%)
    all_gather x1, blocking collectives, per_device(): lax.all_gather(jnp.concatenate([sec, delta_proj], axis=0), 'z', axis=0, t...  115 us
    ppermute x14, waiting for transfers between devices, shift(): return lax.ppermute(value, axis, [(i, (i + k) % size) for i in range(size)])  44.1 us
    reduce_scatter x1, waiting for transfers between devices, per_device(): lax.psum_scatter(partial_mix.astype(BF), ('y', 'c'), scatter_dimension=1,...  34.1 us
    all_gather x1, blocking collectives, per_device(): lax.all_gather(extra.reshape(BASE * STATE, CH), 'z', axis=0, tiled=True)  28.1 us
    all_to_all x1, waiting for transfers between devices, per_device(): lax.all_to_all(buf.reshape(GROUPS, SLOT, CH), ('z', 'x'), split_axis=0, c...  23.4 us
    pallas_call x1, Pallas kernels, scan_stage(): pl.pallas_call(scan_kernel, name='scan', out_shape=(shape((STEPS, ROWS, C...  19.3 us
    ppermute x14, starting transfers between devices, shift(): return lax.ppermute(value, axis, [(i, (i + k) % size) for i in range(size)])  17.8 us
    unnamed x42, local copies, waits for them, and re-layouts  17.6 us
  transfers between devices with their start and end apart: 18, of which 12 were waited for; matrix products, arithmetic and copies ran while one was open for 2% of the time, Pallas kernels for 13%

profile of v1, /device:TPU:40, one launch (start us, length us, event | category | flops | bytes accessed | tf_op | source)
XLA Modules:
  0.0 376.7 jit_solution(3432397282395568432)
XLA Ops:
  7.2 0.0 all-gather.2.cloned.1.call-start
  7.2 0.7 all-gather.2.cloned.1.call-update
  7.9 0.8 dynamic-slice_bitcast_fusion.4.mine_ref
  8.7 0.1 pad_add_fusion.me_ref
  8.8 1.1 copy-done.7
  9.8 0.8 copy-done.12
  10.6 0.7 copy-done.13
  11.3 0.7 copy-done.14
  12.0 2.9 plan.1
  14.9 11.2 %all-to-all-start.1 = ((bf16[32,16,1024]{2,1,0:T(8,128)(2,1)}), bf16[32,16,1024]{2,1,0:T(8,128)(2,1)}, u32[]{:S(2)}, u32[]{:S(2)}) async-start(bf16[32,16,1024]{2,1,0:T(8,128)(2,1)} %bitcast.12), calls=%async_computation.1 | async-start | bytes 2097152 | tf_op jit(solution)/shard_map/all_to_all | solution.py:373
  26.2 0.0 copy-start.1
  26.2 1.9 copy-done.1
  28.1 5.7 %pack.1 = (bf16[96,16,1024]{2,1,0:T(8,128)(2,1)S(1)}, bf16[3,16,1024]{2,1,0:T(8,128)(2,1)S(1)}) custom-call(s32[8,128]{1,0:T(8,128)S(1)} %get-tuple-element.24.pick_ref, bf16[96,16,1024]{2,1,0:T(8,128)(2,1)S(1)} %copy-done.1), custom_call_target="tpu_custom_call" | custom-call | tf_op jit(solution)/shard_map/pack/pallas_call | solution.py:132
  33.8 0.0 copy-start.2
  33.8 1.7 copy-done.2
  35.5 23.4 %all-to-all-done.1 = bf16[32,16,1024]{2,1,0:T(8,128)(2,1)} async-done(((bf16[32,16,1024]{2,1,0:T(8,128)(2,1)}), bf16[32,16,1024]{2,1,0:T(8,128)(2,1)}, u32[]{:S(2)}, u32[]{:S(2)}) %all-to-all-start.1) | async-done | bytes 1048608 | tf_op jit(solution)/shard_map/all_to_all | solution.py:373
  58.9 6.7 %all-to-all-start = ((bf16[96,16,1024]{2,1,0:T(8,128)(2,1)}), bf16[96,16,1024]{2,1,0:T(8,128)(2,1)S(1)}, u32[]{:S(2)}, u32[]{:S(2)}) async-start(bf16[96,16,1024]{2,1,0:T(8,128)(2,1)} %copy-done.2), calls=%async_computation | async-start | bytes 6291456 | tf_op jit(solution)/shard_map/all_to_all | solution.py:381
  65.6 0.0 reduce-scatter.2.cloned.1.call-start
  65.7 114.5 %all_gather.10.g0 = bf16[384,1024]{1,0:T(8,128)(2,1)} all-gather(bf16[48,1024]{1,0:T(8,128)(2,1)S(1)} %pad_maximum_fusion.2), channel_id=1, replica_groups=mesh['z'=8,'x'=4,'y'=4,'c'=2] {'z'}, dimensions={0}, use_global_device_ids=true | all-gather | bytes 884736 | tf_op jit(solution)/shard_map/all_gather | solution.py:377
  180.2 1.9 collective-permute-start.4
  182.2 1.4 collective-permute-start.5
  183.6 15.7 %collective-permute-done.3.g1 = bf16[384,1024]{1,0:T(8,128)(2,1)} collective-permute-done((bf16[384,1024]{1,0:T(8,128)(2,1)}, bf16[384,1024]{1,0:T(8,128)(2,1)}, u32[]{:S(2)}, u32[]{:S(2)}) %collective-permute-start.3) | collective-permute-done | bytes 786464 | tf_op jit(solution)/shard_map/ppermute | solution.py:336
  199.2 12.6 %collective-permute-done.4.g2 = bf16[384,1024]{1,0:T(8,128)(2,1)} collective-permute-done((bf16[384,1024]{1,0:T(8,128)(2,1)}, bf16[384,1024]{1,0:T(8,128)(2,1)}, u32[]{:S(2)}, u32[]{:S(2)}) %collective-permute-start.4) | collective-permute-done | bytes 786464 | tf_op jit(solution)/shard_map/ppermute | solution.py:336
  211.9 9.6 %conv.1 = (f32[4,96,1024]{2,1,0:T(8,128)}, bf16[384,544]{1,0:T(8,128)(2,1)}, bf16[3,96,1024]{2,1,0:T(8,128)(2,1)}) custom-call(s32[4]{0:T(128)} %copy-done.15, bf16[512,1024]{1,0:T(8,128)(2,1)} %bitcast.13.moved_ref, bf16[384,1024]{1,0:T(8,128)(2,1)} %all_gather.10.g0, bf16[384,1024]{1,0:T(8,128)(2,1)} %collective-permute-done.3.g1, ...), custom_call_target="tpu_custom_call" | custom-call | tf_op jit(solution)/shard_map/conv/pallas_call | solution.py:179
  221.4 1.0 dynamic-slice_bitcast_fusion
  222.4 0.1 collective-permute-start.6
  222.5 28.1 %all_gather.9 = bf16[384,1024]{1,0:T(8,128)(2,1)} all-gather(bf16[48,1024]{1,0:T(8,128)(2,1)S(1)} %bitcast.50), channel_id=1, replica_groups=mesh['z'=8,'x'=4,'y'=4,'c'=2] {'z'}, dimensions={0}, use_global_device_ids=true | all-gather | bytes 884736 | tf_op jit(solution)/shard_map/all_gather | solution.py:382
  250.6 1.2 collective-permute-start
  251.8 2.4 collective-permute-start.1
  254.2 1.5 collective-permute-start.2
  255.7 1.1 convert_add_fusion
  256.8 0.8 copy-done.17
  257.6 1.8 collective-permute-start.7
  259.4 0.9 collective-permute-start.8
  260.3 1.8 collective-permute-done.7
  262.1 1.4 collective-permute-start.9
  263.6 1.6 collective-permute-done.8
  265.2 1.5 collective-permute-done.9
  266.7 0.9 fusion.2
  267.6 1.2 collective-permute-start.10
  268.8 2.2 collective-permute-start.11
  271.0 0.9 collective-permute-done.10
  271.9 1.7 collective-permute-start.12
  273.7 0.9 collective-permute-done.11
  274.5 1.6 collective-permute-done.12
  276.1 0.1 pad_maximum_fusion.1.own_ref
  276.2 0.0 copy-start.18
  276.2 0.1 collective-permute-start.13
  276.3 7.2 %collective-permute-done.1 = bf16[8,3,16,1024]{3,2,1,0:T(8,128)(2,1)} collective-permute-done((bf16[8,3,16,1024]{3,2,1,0:T(8,128)(2,1)}, bf16[8,3,16,1024]{3,2,1,0:T(8,128)(2,1)}, u32[]{:S(2)}, u32[]{:S(2)}) %collective-permute-start.1) | collective-permute-done | bytes 786464 | tf_op jit(solution)/shard_map/ppermute | solution.py:336
  283.5 0.3 collective-permute-done.2
  283.8 3.2 pad_maximum_fusion
  287.1 0.7 copy-done.19
  287.7 10.7 %sizes.1 = (f32[4,96,1024]{2,1,0:T(8,128)}, f32[4,96,1024]{2,1,0:T(8,128)}, f32[4,96,1024]{2,1,0:T(8,128)}, f32[4,96,1024]{2,1,0:T(8,128)}, f32[4,32,96,128]{3,2,1,0:T(8,128)}, /*index=5*/f32[16,1024]{1,0:T(8,128)}) custom-call(s32[4]{0:T(128)} %copy-done.15, bf16[4,48,544]{2,1,0:T(8,128)(2,1)} %copy-done.18, bf16[4,48,544]{2,1,0:T(8,128)(2,1)} %copy-done.19, ...), custom_call_target="tpu_custom_call" | custom-call | tf_op jit(solution)/shard_map/sizes/pallas_call | solution.py:234
  298.5 1.9 copy-done
  300.4 1.4 copy-done.3
  301.8 1.4 copy-done.4
  303.2 1.4 copy-done.5
  304.6 1.4 copy-done.6
  306.0 0.8 copy-done.11
  306.9 19.3 %scan.1 = (bf16[4,96,1024]{2,1,0:T(8,128)(2,1)S(1)}, bf16[96,16,1024]{2,1,0:T(8,128)(2,1)}) custom-call(s32[1,96]{1,0:T(1,128)S(1)} %compare_select_fusion.at_ref, bf16[96,16,1024]{2,1,0:T(8,128)(2,1)S(1)} %all-to-all-done.main_ref, bf16[96,16,1024]{2,1,0:T(8,128)(2,1)S(1)} %bitcast.48, f32[4,96,1024]{2,1,0:T(8,128)S(1)} %copy-done.3, ...), custom_call_target="tpu_custom_call" | custom-call | tf_op jit(solution)/shard_map/scan/pallas_call | solution.py:307
  326.2 0.9 copy-done.16
  327.1 8.7 %convolution_convert_fusion = bf16[384,4096]{1,0:T(8,128)(2,1)} fusion(bf16[384,1024]{1,0:T(8,128)(2,1)} %bitcast.54, bf16[1024,4096]{1,0:T(8,128)(2,1)} %all-gather.2.cloned.1.call-done), kind=kOutput, calls=%fused_computation | convolution fusion | flops 3222798336 | bytes 12320768 | tf_op jit(solution)/shard_map/dot_general | solution.py:39
  335.8 0.0 reduce-scatter.2.cloned.1.call-update
  335.8 34.1 %reduce-scatter.2.cloned.1.call-done = bf16[384,512]{1,0:T(8,128)(2,1)} async-done(((bf16[384,4096]{1,0:T(8,128)(2,1)}), bf16[384,512]{1,0:T(8,128)(2,1)}) %reduce-scatter.2.cloned.1.call-update) | async-done | bytes 393232 | tf_op jit(solution)/shard_map/reduce_scatter | solution.py:400
  (35 shorter events, 0.2 us)
Async XLA Ops:
  7.2 319.9 %all-gather.2.cloned.1.call-start = ((), (), s32[]{:S(2)}) async-start(), calls=%async_computation.3 | async-start | bytes 8650752 | tf_op jit(solution)/shard_map/all_gather | solution.py:363
  8.8 50.1 %copy-start.15 = (s32[4]{0:T(128)}, s32[4]{0:T(128)S(1)}, u32[]{:S(2)}) copy-start(s32[4]{0:T(128)S(1)} %pad_add_fusion.me_ref) | copy-start | bytes 52
  8.8 1.1 copy-start.7
  9.8 0.8 copy-start.12
  10.6 0.7 copy-start.13
  11.3 0.7 copy-start.14
  14.9 11.3 %copy-start.8 = (s32[96,1]{1,0:T(8,128)}, s32[96,1]{1,0:T(8,128)S(1)}, u32[]{:S(2)}) copy-start(s32[96,1]{1,0:T(8,128)S(1)} %get-tuple-element.31.rem_ref) | copy-start | bytes 1156
  14.9 11.3 %copy-start.9 = (s32[288,1]{1,0:T(8,128)}, s32[288,1]{1,0:T(8,128)S(1)}, u32[]{:S(2)}) copy-start(s32[288,1]{1,0:T(8,128)S(1)} %get-tuple-element.29.col_ref) | copy-start | bytes 3460
  14.9 11.3 %copy-start.10 = (s32[288,1]{1,0:T(8,128)}, s32[288,1]{1,0:T(8,128)S(1)}, u32[]{:S(2)}) copy-start(s32[288,1]{1,0:T(8,128)S(1)} %get-tuple-element.30.ext_ref) | copy-start | bytes 3460
  14.9 44.0 %all-to-all-start.1 = ((bf16[32,16,1024]{2,1,0:T(8,128)(2,1)}), bf16[32,16,1024]{2,1,0:T(8,128)(2,1)}, u32[]{:S(2)}, u32[]{:S(2)}) async-start(bf16[32,16,1024]{2,1,0:T(8,128)(2,1)} %bitcast.12), calls=%async_computation.1 | async-start | bytes 2097152 | tf_op jit(solution)/shard_map/all_to_all | solution.py:373
  26.2 1.9 copy-start.1
  33.8 1.7 copy-start.2
  58.9 6.8 %copy-start.20 = (bf16[16,1024]{1,0:T(8,128)(2,1)S(1)}, bf16[16,1024]{1,0:T(8,128)(2,1)}, u32[]{:S(2)}) copy-start(bf16[16,1024]{1,0:T(8,128)(2,1)} %param.23) | copy-start | bytes 98308
  58.9 239.6 %all-to-all-start = ((bf16[96,16,1024]{2,1,0:T(8,128)(2,1)}), bf16[96,16,1024]{2,1,0:T(8,128)(2,1)S(1)}, u32[]{:S(2)}, u32[]{:S(2)}) async-start(bf16[96,16,1024]{2,1,0:T(8,128)(2,1)} %copy-done.2), calls=%async_computation | async-start | bytes 6291456 | tf_op jit(solution)/shard_map/all_to_all | solution.py:381
  65.6 304.3 %reduce-scatter.2.cloned.1.call-start = ((), (), s32[]{:S(2)}) async-start(), calls=%async_computation.4 | async-start | bytes 3538944 | tf_op jit(solution)/shard_map/reduce_scatter | solution.py:400
  180.2 19.0 %collective-permute-start.3 = (bf16[384,1024]{1,0:T(8,128)(2,1)}, bf16[384,1024]{1,0:T(8,128)(2,1)}, u32[]{:S(2)}, u32[]{:S(2)}) collective-permute-start(bf16[384,1024]{1,0:T(8,128)(2,1)} %all_gather.10.g0), channel_id=1, source_target_pairs={{0,8},{8,16},{16,24},{24,0},{1,9},{9,17},{17,25},{25,1},{2,10},{10... | collective-permute-start | bytes 2359304 | tf_op jit(solution)/shard_map/ppermute | solution.py:336
  180.2 31.6 %collective-permute-start.4 = (bf16[384,1024]{1,0:T(8,128)(2,1)}, bf16[384,1024]{1,0:T(8,128)(2,1)}, u32[]{:S(2)}, u32[]{:S(2)}) collective-permute-start(bf16[384,1024]{1,0:T(8,128)(2,1)} %all_gather.10.g0), channel_id=1, source_target_pairs={{0,16},{8,24},{16,0},{24,8},{1,17},{9,25},{17,1},{25,9},{2,18},{10... | collective-permute-start | bytes 2359304 | tf_op jit(solution)/shard_map/ppermute | solution.py:336
  182.2 29.7 %collective-permute-start.5 = (bf16[384,1024]{1,0:T(8,128)(2,1)}, bf16[384,1024]{1,0:T(8,128)(2,1)}, u32[]{:S(2)}, u32[]{:S(2)}) collective-permute-start(bf16[384,1024]{1,0:T(8,128)(2,1)} %all_gather.10.g0), channel_id=1, source_target_pairs={{0,24},{8,0},{16,8},{24,16},{1,25},{9,1},{17,9},{25,17},{2,26},{10... | collective-permute-start | bytes 2359304 | tf_op jit(solution)/shard_map/ppermute | solution.py:336
  222.4 33.3 %collective-permute-start.6 = (bf16[192,544]{1,0:T(8,128)(2,1)S(1)}, bf16[192,544]{1,0:T(8,128)(2,1)}, u32[]{:S(2)}, u32[]{:S(2)}) collective-permute-start(bf16[192,544]{1,0:T(8,128)(2,1)S(1)} %dynamic-slice_bitcast_fusion), channel_id=1, source_target_pairs={{0,1},{1,0},{2,3},{3,2},{4,5},{5,4},{6,7},{7,6},{8,9},{9,8},{10,11... | collective-permute-start | bytes 626696 | tf_op jit(solution)/shard_map/ppermute | solution.py:336
  250.6 25.7 %collective-permute-start = (bf16[8,3,16,1024]{3,2,1,0:T(8,128)(2,1)}, bf16[8,3,16,1024]{3,2,1,0:T(8,128)(2,1)}, u32[]{:S(2)}, u32[]{:S(2)}) collective-permute-start(bf16[8,3,16,1024]{3,2,1,0:T(8,128)(2,1)} %bitcast.10), channel_id=1, source_target_pairs={{0,8},{8,16},{16,24},{24,0},{1,9},{9,17},{17,25},{25,1},{2,10},{10... | collective-permute-start | bytes 2359304 | tf_op jit(solution)/shard_map/ppermute | solution.py:336
  251.8 31.7 %collective-permute-start.1 = (bf16[8,3,16,1024]{3,2,1,0:T(8,128)(2,1)}, bf16[8,3,16,1024]{3,2,1,0:T(8,128)(2,1)}, u32[]{:S(2)}, u32[]{:S(2)}) collective-permute-start(bf16[8,3,16,1024]{3,2,1,0:T(8,128)(2,1)} %bitcast.10), channel_id=1, source_target_pairs={{0,16},{8,24},{16,0},{24,8},{1,17},{9,25},{17,1},{25,9},{2,18},{10... | collective-permute-start | bytes 2359304 | tf_op jit(solution)/shard_map/ppermute | solution.py:336
  254.2 29.6 %collective-permute-start.2 = (bf16[8,3,16,1024]{3,2,1,0:T(8,128)(2,1)}, bf16[8,3,16,1024]{3,2,1,0:T(8,128)(2,1)}, u32[]{:S(2)}, u32[]{:S(2)}) collective-permute-start(bf16[8,3,16,1024]{3,2,1,0:T(8,128)(2,1)} %bitcast.10), channel_id=1, source_target_pairs={{0,24},{8,0},{16,8},{24,16},{1,25},{9,1},{17,9},{25,17},{2,26},{10... | collective-permute-start | bytes 2359304 | tf_op jit(solution)/shard_map/ppermute | solution.py:336
  256.8 0.8 copy-start.17
  257.6 4.5 %collective-permute-start.7 = (bf16[48,544]{1,0:T(8,128)(2,1)S(1)}, bf16[48,544]{1,0:T(8,128)(2,1)S(1)}, u32[]{:S(2)}, u32[]{:S(2)}) collective-permute-start(bf16[48,544]{1,0:T(8,128)(2,1)S(1)} %get-tuple-element.43), channel_id=1, source_target_pairs={{0,2},{2,4},{4,6},{6,0},{1,3},{3,5},{5,7},{7,1},{8,10},{10,12},{12... | collective-permute-start | bytes 156680 | tf_op jit(solution)/shard_map/ppermute | solution.py:336
  259.4 5.7 %collective-permute-start.8 = (bf16[48,544]{1,0:T(8,128)(2,1)S(1)}, bf16[48,544]{1,0:T(8,128)(2,1)S(1)}, u32[]{:S(2)}, u32[]{:S(2)}) collective-permute-start(bf16[48,544]{1,0:T(8,128)(2,1)S(1)} %get-tuple-element.45), channel_id=1, source_target_pairs={{0,4},{2,6},{4,0},{6,2},{1,5},{3,7},{5,1},{7,3},{8,12},{10,14},{12... | collective-permute-start | bytes 156680 | tf_op jit(solution)/shard_map/ppermute | solution.py:336
  262.1 4.5 %collective-permute-start.9 = (bf16[48,544]{1,0:T(8,128)(2,1)S(1)}, bf16[48,544]{1,0:T(8,128)(2,1)S(1)}, u32[]{:S(2)}, u32[]{:S(2)}) collective-permute-start(bf16[48,544]{1,0:T(8,128)(2,1)S(1)} %get-tuple-element.44), channel_id=1, source_target_pairs={{0,6},{2,0},{4,2},{6,4},{1,7},{3,1},{5,3},{7,5},{8,14},{10,8},{12,... | collective-permute-start | bytes 156680 | tf_op jit(solution)/shard_map/ppermute | solution.py:336
  267.6 4.3 %collective-permute-start.10 = (bf16[48,544]{1,0:T(8,128)(2,1)S(1)}, bf16[48,544]{1,0:T(8,128)(2,1)S(1)}, u32[]{:S(2)}, u32[]{:S(2)}) collective-permute-start(bf16[48,544]{1,0:T(8,128)(2,1)S(1)} %fusion.2), channel_id=1, source_target_pairs={{0,6},{2,0},{4,2},{6,4},{1,7},{3,1},{5,3},{7,5},{8,14},{10,8},{12,... | collective-permute-start | bytes 156680 | tf_op jit(solution)/shard_map/ppermute | solution.py:336
  268.8 5.7 %collective-permute-start.11 = (bf16[48,544]{1,0:T(8,128)(2,1)S(1)}, bf16[48,544]{1,0:T(8,128)(2,1)S(1)}, u32[]{:S(2)}, u32[]{:S(2)}) collective-permute-start(bf16[48,544]{1,0:T(8,128)(2,1)S(1)} %fusion.2), channel_id=1, source_target_pairs={{0,4},{2,6},{4,0},{6,2},{1,5},{3,7},{5,1},{7,3},{8,12},{10,14},{12... | collective-permute-start | bytes 156680 | tf_op jit(solution)/shard_map/ppermute | solution.py:336
  271.9 4.2 %collective-permute-start.12 = (bf16[48,544]{1,0:T(8,128)(2,1)S(1)}, bf16[48,544]{1,0:T(8,128)(2,1)S(1)}, u32[]{:S(2)}, u32[]{:S(2)}) collective-permute-start(bf16[48,544]{1,0:T(8,128)(2,1)S(1)} %fusion.2), channel_id=1, source_target_pairs={{0,2},{2,4},{4,6},{6,0},{1,3},{3,5},{5,7},{7,1},{8,10},{10,12},{12... | collective-permute-start | bytes 156680 | tf_op jit(solution)/shard_map/ppermute | solution.py:336
  276.2 10.9 %copy-start.18 = (bf16[4,48,544]{2,1,0:T(8,128)(2,1)}, bf16[4,48,544]{2,1,0:T(8,128)(2,1)S(1)}, u32[]{:S(2)}) copy-start(bf16[4,48,544]{2,1,0:T(8,128)(2,1)S(1)} %pad_maximum_fusion.1.own_ref) | copy-start | bytes 626692
  276.2 10.9 %collective-permute-start.13 = (bf16[4,48,544]{2,1,0:T(8,128)(2,1)S(1)}, bf16[4,48,544]{2,1,0:T(8,128)(2,1)S(1)}, u32[]{:S(2)}, u32[]{:S(2)}) collective-permute-start(bf16[4,48,544]{2,1,0:T(8,128)(2,1)S(1)} %pad_maximum_fusion.1.own_ref), channel_id=1, source_target_pairs={{0,1},{1,0},{2,3},{3,2},{4,5},{5,4},{6,7},{7,6},{8,9},{9,8},{10,11... | collective-permute-start | bytes 626696 | tf_op jit(solution)/shard_map/ppermute | solution.py:336
  287.0 0.7 copy-start.19
  298.5 1.9 copy-start
  300.4 1.4 copy-start.3
  301.8 1.4 copy-start.4
  303.2 1.4 copy-start.5
  304.6 1.4 copy-start.6
  306.0 0.8 copy-start.11
  326.2 0.9 copy-start.16
Sparse Core Ops, SparseCore 0:
  10.5 176.5 all-gather.1
  335.9 33.9 reduce-scatter.1

commit v2 on v1

--- a/solution.py
+++ b/solution.py
@@ -48,34 +48,17 @@
 
 
 def plan_kernel(
-    me_ref, slots_ref, remaining_ref, mine_ref, conv_ref, coef_ref,
-    pack_ref, gather_ref, rem_ref, col_ref, ext_ref, buf_ref, sec_ref,
+    me_ref, slots_ref, remaining_ref, table_ref, conv_ref, coef_ref, delta_ref, ssm_ref, proj_ref,
+    gather_ref, relay_ref, rem_ref, col_ref, ext_ref, buf_ref, block_ref, main_ref, proj_out_ref,
+    pick_ref, pick_smem, sems,
 ):
     me = me_ref[0]
-    match = (slots_ref[...] == me * ROWS + iota((ROWS, GROUPS * ROWS), 0)).astype(I32)
-    inv = jnp.sum(match * iota(match.shape, 1), axis=1, keepdims=True)
-    rem_ref[...] = jnp.sum(match * remaining_ref[...], axis=1, keepdims=True)
+    x = me_ref[1]
+    passed = pltpu.make_async_copy(proj_ref, proj_out_ref, sems.at[3])
+    passed.start()
     square = (ROWS, ROWS)
     eye = iota(square, 0) == iota(square, 1)
-    inv_row = jnp.sum(jnp.where(eye, inv, 0), axis=0, keepdims=True)
-    src = inv // ROWS
-    src_row = inv_row // ROWS
-    rank = jnp.sum(
-        ((src == src_row) & (inv_row < inv)).astype(I32), axis=1, keepdims=True
-    )
-    rank_row = jnp.sum(
-        ((src == src_row) & (inv < inv_row)).astype(I32), axis=0, keepdims=True
-    )
-    base_row = src_row * BASE + rank_row
-    where_row = jnp.where(rank_row < BASE, base_row, ROWS + base_row - BASE)
-    gather_ref[...] = jnp.broadcast_to(where_row, gather_ref.shape)
-    for tap in range(3):
-        at = pl.ds(tap * ROWS, ROWS)
-        col_ref[at, :] = jnp.where(rank < BASE, src * SLOT + rank * 3 + tap, -1)
-        ext_ref[at, :] = jnp.where(
-            rank < BASE, -1, src * GATH + COEF + (rank - BASE) * 3 + tap
-        )
-    to_row = mine_ref[...] // ROWS
+    to_row = table_ref[pl.ds(me, 1), :] // ROWS
     to = jnp.sum(jnp.where(eye, to_row, 0), axis=1, keepdims=True)
     same = to == to_row
     order_row = jnp.sum((same & (iota(square, 0) < iota(square, 1))).astype(I32), axis=0, keepdims=True)
@@ -83,7 +66,20 @@
     place = jnp.where(order < BASE, to * BASE + order, ROWS + order - BASE)
     lanes = (ROWS, 128)
     picked = jnp.sum(jnp.where(place == iota(lanes, 1), iota(lanes, 0), 0), axis=0, keepdims=True)
-    pack_ref[...] = jnp.broadcast_to(picked, pack_ref.shape)
+    pick_ref[...] = jnp.broadcast_to(picked, pick_ref.shape)
+    picking = pltpu.make_async_copy(pick_ref, pick_smem, sems.at[0])
+    picking.start()
+    picking.wait()
+    for p in range(BASE):
+        pltpu.make_async_copy(
+            ssm_ref.at[pick_smem[0, ROWS + p]], block_ref.at[pl.ds(GATH + p * STATE, STATE)], sems.at[2]
+        ).start()
+
+    def send(p, carry):
+        pltpu.make_async_copy(ssm_ref.at[pick_smem[0, p]], main_ref.at[p], sems.at[1]).start()
+        return carry
+
+    lax.fori_loop(0, ROWS, send, 0)
     buf = jnp.zeros((GROUPS * SLOT, CH), F32)
     sec = bdot(onehot(iota((SEC, COEF), 0) == iota((SEC, COEF), 1)), coef_ref[...])
     for tap in range(3):
@@ -92,52 +88,69 @@
         dest = jnp.where(order_row < BASE, -1, COEF + (order_row - BASE) * 3 + tap)
         sec += bdot(onehot(iota((SEC, ROWS), 0) == dest), conv_ref[tap])
     buf_ref[...] = buf.astype(BF)
-    sec_ref[...] = sec.astype(BF)
-
-
-def plan(me, slots, remaining, mine, conv, coef):
+    block_ref[pl.ds(0, SEC), :] = sec.astype(BF)
+    block_ref[pl.ds(SEC, DELTA), :] = delta_ref[...]
+    match = (slots_ref[...] == me * ROWS + iota((ROWS, GROUPS * ROWS), 0)).astype(I32)
+    inv = jnp.sum(match * iota(match.shape, 1), axis=1, keepdims=True)
+    rem_ref[...] = jnp.sum(match * remaining_ref[...], axis=1, keepdims=True)
+    inv_row = jnp.sum(jnp.where(eye, inv, 0), axis=0, keepdims=True)
+    src = inv // ROWS
+    src_row = inv_row // ROWS
+    rank = jnp.sum(
+        ((src == src_row) & (inv_row < inv)).astype(I32), axis=1, keepdims=True
+    )
+    rank_row = jnp.sum(
+        ((src == src_row) & (inv < inv_row)).astype(I32), axis=0, keepdims=True
+    )
+    turn = lax.rem(x - lax.rem(src_row, NX) + NX, NX)
+    where_row = jnp.where(rank_row < BASE, src_row * BASE + rank_row, ROWS + (turn - 1) * BASE + rank_row)
+    gather_ref[...] = jnp.broadcast_to(where_row, gather_ref.shape)
+    for tap in range(3):
+        at = pl.ds(tap * ROWS, ROWS)
+        col_ref[at, :] = jnp.where(rank < BASE, src * SLOT + rank * 3 + tap, -1)
+        ext_ref[at, :] = jnp.where(
+            rank < BASE, -1, src * SEC + COEF + (rank - BASE) * 3 + tap
+        )
+    target = table_ref[...] // ROWS
+    groups = iota((GROUPS, 1), 0)
+    for k in range(NX):
+        dest = me - x + lax.rem(x + k, NX)
+        count = jnp.sum((target == dest).astype(I32), axis=1, keepdims=True)
+        holds = (count > BASE) & (lax.rem(groups, NX) == x)
+        z = jnp.sum(jnp.where(holds, groups // NX, 0), axis=0, keepdims=True)
+        relay_ref[pl.ds(k, 1), :] = jnp.broadcast_to(z, (1, 128))
+    pltpu.make_async_copy(
+        ssm_ref.at[pl.ds(0, BASE)].reshape(BASE * STATE, CH), block_ref.at[pl.ds(GATH, BASE * STATE)], sems.at[2]
+    ).wait()
+    pltpu.make_async_copy(ssm_ref, main_ref, sems.at[1]).wait()
+    passed.wait()
+
+
+def plan(me, slots, remaining, table, conv, coef, delta, ssm, proj):
     shape = jax.ShapeDtypeStruct
     return pl.pallas_call(
         plan_kernel,
         name="plan",
         out_shape=(
-            shape((8, 128), I32),
             shape((8, ROWS), I32),
+            shape((NX, 128), I32),
             shape((ROWS, 1), I32),
             shape((3 * ROWS, 1), I32),
             shape((3 * ROWS, 1), I32),
             shape((GROUPS * SLOT, CH), BF),
-            shape((SEC, CH), BF),
+            shape((GATH + BASE * STATE, CH), BF),
+            shape((ROWS, STATE, CH), BF),
+            shape(proj.shape, BF),
         ),
-        in_specs=[SMEM] + [VMEM] * 5,
-        out_specs=(VMEM,) * 7,
-        compiler_params=pltpu.CompilerParams(vmem_limit_bytes=40 << 20),
-    )(me, slots, remaining, mine, conv, coef)
-
-
-def pack_kernel(pick_ref, ssm_ref, main_ref, extra_ref, sems):
-    def send(p, carry):
-        pltpu.make_async_copy(ssm_ref.at[pick_ref[0, p]], main_ref.at[p], sems.at[0]).start()
-        return carry
-
-    lax.fori_loop(0, ROWS, send, 0)
-    for p in range(BASE):
-        pltpu.make_async_copy(ssm_ref.at[pick_ref[0, ROWS + p]], extra_ref.at[p], sems.at[1]).start()
-    pltpu.make_async_copy(ssm_ref, main_ref, sems.at[0]).wait()
-    pltpu.make_async_copy(ssm_ref.at[pl.ds(0, BASE)], extra_ref, sems.at[1]).wait()
-
-
-def pack(pick, ssm):
-    shape = jax.ShapeDtypeStruct
-    return pl.pallas_call(
-        pack_kernel,
-        name="pack",
-        out_shape=(shape((ROWS, STATE, CH), BF), shape((BASE, STATE, CH), BF)),
-        in_specs=[SMEM, ANY],
-        out_specs=(ANY, ANY),
-        scratch_shapes=[pltpu.SemaphoreType.DMA((2,))],
-        compiler_params=pltpu.CompilerParams(vmem_limit_bytes=8 << 20),
-    )(pick, ssm)
+        in_specs=[SMEM] + [VMEM] * 6 + [ANY] * 2,
+        out_specs=(VMEM,) * 7 + (ANY,) * 2,
+        scratch_shapes=[
+            pltpu.VMEM((8, 128), I32),
+            pltpu.SMEM((8, 128), I32),
+            pltpu.SemaphoreType.DMA((4,)),
+        ],
+        compiler_params=pltpu.CompilerParams(vmem_limit_bytes=60 << 20),
+    )(me, slots, remaining, table, conv, coef, delta, ssm, proj)
 
 
 def conv_kernel(
@@ -146,14 +159,14 @@
 ):
     x = me_ref[1]
     parts = (g0, g1, g2, g3)
-    span = NZ * GATH
+    span = NZ * SEC
     window = bdot(onehot(col_ref[...] == iota((3 * ROWS, GROUPS * SLOT), 1)), moved_ref[...])
     coef = jnp.zeros((LOW, CH), F32)
     for k, part in enumerate(parts):
         at = iota((1, span), 1)
-        z, q = at // GATH, at % GATH
+        z, q = at // SEC, at % SEC
         group = z * NX + lax.rem(x - k + NX, NX)
-        ext = onehot(ext_ref[...] == group * GATH + q)
+        ext = onehot(ext_ref[...] == group * SEC + q)
         window += bdot(ext, part[...])
         row = jnp.where(q < COEF, group * COEF + q, -1)
         coef += bdot(onehot(iota((LOW, span), 0) == row), part[...])
@@ -186,7 +199,7 @@
         ),
         in_specs=[SMEM] + [VMEM] * 11,
         out_specs=(VMEM,) * 3,
-        compiler_params=pltpu.CompilerParams(vmem_limit_bytes=56 << 20),
+        compiler_params=pltpu.CompilerParams(vmem_limit_bytes=60 << 20),
     )(me, moved, *parts, col, ext, rem, inputs, weight, bias)
 
 
@@ -201,13 +214,12 @@
         for m in range(NY):
             at = half * NY + lax.rem(y + m, NY)
             low_ref[pl.ds(pl.multiple_of(at * chunk, 16), chunk), :] = piece[m]
-    span = NZ * GATH
+    span = NZ * DELTA
     delta = jnp.zeros((RANK, CH), F32)
     for k, part in enumerate((g0, g1, g2, g3)):
         at = iota((1, span), 1)
-        z, q = at // GATH, at % GATH
-        group = z * NX + lax.rem(x - k + NX, NX)
-        row = jnp.where(q >= SEC, group * DELTA + q - SEC, -1)
+        z, q = at // DELTA, at % DELTA
+        row = (z * NX + lax.rem(x - k + NX, NX)) * DELTA + q
         delta += bdot(onehot(iota((RANK, span), 0) == row), part[...])
     delta = delta.astype(BF)
     rem = rem_ref[...]
@@ -238,7 +250,7 @@
         in_specs=[SMEM] + [VMEM] * 12,
         out_specs=(VMEM,) * 6,
         scratch_shapes=[pltpu.VMEM((STEPS * ROWS, LOW), BF)],
-        compiler_params=pltpu.CompilerParams(vmem_limit_bytes=56 << 20),
+        compiler_params=pltpu.CompilerParams(vmem_limit_bytes=60 << 20),
     )(me, own, other, *parts, bias, act, gate, skip, rem, log)
 
 
@@ -247,7 +259,7 @@
 
 
 def scan_kernel(
-    at_ref, main_ref, extra_ref, dt_ref, dx_ref, sk_ref, sg_ref, bc_ref, rate_ref,
+    at_ref, main_ref, e0, e1, e2, e3, dt_ref, dx_ref, sk_ref, sg_ref, bc_ref, rate_ref,
     out_ref, final_ref, held, wide, sems,
 ):
     b = pl.program_id(0)
@@ -260,9 +272,12 @@
             def _():
                 pltpu.make_async_copy(main_ref.at[at], held.at[block, i], sems.at[block]).start()
 
-            @pl.when(at >= ROWS)
-            def _():
-                pltpu.make_async_copy(extra_ref.at[at - ROWS], held.at[block, i], sems.at[block]).start()
+            for k, extra in enumerate((e0, e1, e2, e3)):
+                row = at - ROWS - k * BASE
+
+                @pl.when((row >= 0) & (row < BASE))
+                def _(row=row, extra=extra):
+                    pltpu.make_async_copy(extra.at[row], held.at[block, i], sems.at[block]).start()
 
     @pl.when(b == 0)
     def _():
@@ -301,7 +316,7 @@
             final_ref[i, :, pl.ds(l * 128, 128)] = wide[l, pl.ds(i * STATE, STATE), :].astype(BF)
 
 
-def scan_stage(at, main, extra, dt, dx, sk, sg, bc, rate):
+def scan_stage(at, main, extras, dt, dx, sk, sg, bc, rate):
     shape = jax.ShapeDtypeStruct
     rows = pl.BlockSpec((STEPS, BLOCK, CH), lambda b, at: (0, b, 0))
     return pl.pallas_call(
@@ -312,6 +327,9 @@
             num_scalar_prefetch=1,
             grid=(BLOCKS,),
             in_specs=[
+                ANY,
+                ANY,
+                ANY,
                 ANY,
                 ANY,
                 rows,
@@ -328,8 +346,8 @@
                 pltpu.SemaphoreType.DMA((BLOCKS,)),
             ],
         ),
-        compiler_params=pltpu.CompilerParams(vmem_limit_bytes=40 << 20),
-    )(at, main, extra, dt, dx, sk, sg, bc, rate)
+        compiler_params=pltpu.CompilerParams(vmem_limit_bytes=60 << 20),
+    )(at, main, *extras, dt, dx, sk, sg, bc, rate)
 
 
 def shift(value, axis, size, k):
@@ -360,42 +378,42 @@
     z, x, y, c = (lax.axis_index(name) for name in ("z", "x", "y", "c"))
     group = z * NX + x
     me = jnp.stack([group, x, y, c]).astype(I32)
-    out_whole = lax.all_gather(out_proj, ("z", "x"), axis=1, tiled=True)
-    mine = lax.dynamic_slice_in_dim(new_slot, group * ROWS, ROWS)
-    pick, at, rem, col, ext, buf, sec = plan(
+    at, relay, rem, col, ext, buf, block, main, proj = plan(
         me,
         new_slot.reshape(1, -1),
         remaining.reshape(1, -1),
-        mine.reshape(1, -1),
+        new_slot.reshape(GROUPS, ROWS),
         conv_state.transpose(1, 0, 2),
         coef_proj.T,
-    )
+        delta_proj,
+        ssm_state,
+        out_proj,
+    )
+    gathered = lax.all_gather(block, "z", axis=0)
     moved = lax.all_to_all(
         buf.reshape(GROUPS, SLOT, CH), ("z", "x"), split_axis=0, concat_axis=0, tiled=True
     ).reshape(GROUPS * SLOT, CH)
-    main, extra = pack(pick, ssm_state)
-    gathered = lax.all_gather(
-        jnp.concatenate([sec, delta_proj], axis=0), "z", axis=0, tiled=True
-    )
-    parts = [gathered] + [shift(gathered, "x", NX, k) for k in range(1, NX)]
+    out_whole = lax.all_gather(proj, ("z", "x"), axis=1, tiled=True)
     ssm_main = lax.all_to_all(main, ("z", "x"), split_axis=0, concat_axis=0, tiled=True)
-    extras = lax.all_gather(extra.reshape(BASE * STATE, CH), "z", axis=0, tiled=True)
-    extras = extras.reshape(NZ, BASE, STATE, CH)
-    extras = [extras] + [shift(extras, "x", NX, k) for k in range(1, NX)]
+
+    def turned(value):
+        return [value] + [shift(value, "x", NX, k) for k in range(1, NX)]
+
+    secs = turned(gathered[:, :SEC].reshape(NZ * SEC, CH))
+    deltas = turned(gathered[:, SEC:GATH].reshape(NZ * DELTA, CH))
+    extras = [
+        lax.dynamic_slice(gathered, (relay[k, 0], GATH, 0), (1, BASE * STATE, CH)) for k in range(NX)
+    ]
+    extras = [extras[0]] + [shift(extras[k], "x", NX, k) for k in range(1, NX)]
+    extras = [e.reshape(BASE, STATE, CH) for e in extras]
     act, low, conv_final = conv_stage(
-        me, moved, parts, col, ext, rem, input_steps, conv_weight, conv_bias.reshape(1, -1)
+        me, moved, secs, col, ext, rem, input_steps, conv_weight, conv_bias.reshape(1, -1)
     )
     own, other = reduce_mp(low, y, c)
     dt, dx, sk, sg, bc, rate = step_stage(
-        me, own, other, parts, delta_bias.reshape(1, -1), act, gate_steps, skip_gain.reshape(1, -1), rem, decay_log
-    )
-    spot = at[:1] - ROWS
-    their = spot // BASE
-    turned = (lax.rem(x - their % NX + NX, NX) * NZ + their // NX) * BASE + spot % BASE
-    at = jnp.where(at[:1] < ROWS, at[:1], ROWS + turned)
-    stepped, ssm_final = scan_stage(
-        at, ssm_main, jnp.concatenate(extras, axis=0).reshape(ROWS, STATE, CH), dt, dx, sk, sg, bc, rate
-    )
+        me, own, other, deltas, delta_bias.reshape(1, -1), act, gate_steps, skip_gain.reshape(1, -1), rem, decay_log
+    )
+    stepped, ssm_final = scan_stage(at, ssm_main, extras, dt, dx, sk, sg, bc, rate)
     partial_mix = bdot(stepped.reshape(STEPS * ROWS, CH), out_whole)
     summed = lax.psum_scatter(partial_mix.astype(BF), ("y", "c"), scatter_dimension=1, tiled=True)
     return summed.reshape(STEPS, ROWS, -1), conv_final.transpose(1, 0, 2), ssm_final

time: 381 us -> 376 us (0.987)
  blocking collectives: 143 us -> 49 us
  Pallas kernels: 48.1 us -> 140 us
  local copies, waits for them, and re-layouts: 19.4 us -> 11.5 us
  between operations: 14.3 us -> 21 us
  starting transfers between devices: 35.8 us -> 29.9 us
  waiting for transfers between devices: 102 us -> 107 us
    all_gather x2 -> x0, blocking collectives: 143 us -> none  [the longest x1 115 us: per_device(): lax.all_gather(jnp.concatenate([sec, delta_proj], axis=0), 'z', axis=0, t...]
    pallas_call x2 -> x1, Pallas kernels: 8.53 us -> 107 us  [plan(): pl.pallas_call(plan_kernel, name='plan', out_shape=(shape((8, ROWS), I32)...]
    all_to_all x0 -> x1, blocking collectives: none -> 49 us  [per_device(): lax.all_to_all(buf.reshape(GROUPS, SLOT, CH), ('z', 'x'), split_axis=0, c...]
    all_to_all x1 -> x0, waiting for transfers between devices: 23.4 us -> none  [per_device(): lax.all_to_all(buf.reshape(GROUPS, SLOT, CH), ('z', 'x'), split_axis=0, c...]
    all_gather x1 -> x2, waiting for transfers between devices: 0.01 us -> 16.8 us  [the longest x1 16.8 us: per_device(): out_whole = lax.all_gather(proj, ('z', 'x'), axis=1, tiled=True)]
    unnamed x42 -> x16, local copies, waits for them, and re-layouts: 17.6 us -> 3.22 us
    ppermute x14 -> x17, waiting for transfers between devices: 44.1 us -> 55.9 us  [shift(): return lax.ppermute(value, axis, [(i, (i + k) % size) for i in range(size)])]
    all_to_all x1 -> x0, starting transfers between devices: 11.2 us -> none  [per_device(): lax.all_to_all(buf.reshape(GROUPS, SLOT, CH), ('z', 'x'), split_axis=0, c...]
  transfers between devices with their start and end apart: 18 -> 21, of which waited for: 12 -> 7; matrix products, arithmetic and copies ran while one was open for 2% -> 3% of each run, Pallas kernels for 13% -> 9%
where the time goes in v2:
time: 376 us; the launch traced here: 371 us
  Pallas kernels  140 us (37%)
  waiting for transfers between devices  107 us (28%)
  blocking collectives  49 us (13%)
  starting transfers between devices  29.9 us (8%)
  between operations  21 us (6%)
  local copies, waits for them, and re-layouts  11.5 us (3%)
  matrix products  8.69 us (2%)
    pallas_call x1, Pallas kernels, plan(): pl.pallas_call(plan_kernel, name='plan', out_shape=(shape((8, ROWS), I32)...  107 us
    ppermute x17, waiting for transfers between devices, shift(): return lax.ppermute(value, axis, [(i, (i + k) % size) for i in range(size)])  55.9 us
    all_to_all x1, blocking collectives, per_device(): lax.all_to_all(buf.reshape(GROUPS, SLOT, CH), ('z', 'x'), split_axis=0, c...  49 us
    reduce_scatter x1, waiting for transfers between devices, per_device(): lax.psum_scatter(partial_mix.astype(BF), ('y', 'c'), scatter_dimension=1,...  33.9 us
    ppermute x17, starting transfers between devices, shift(): return lax.ppermute(value, axis, [(i, (i + k) % size) for i in range(size)])  23.6 us
    all_gather x1, waiting for transfers between devices, per_device(): out_whole = lax.all_gather(proj, ('z', 'x'), axis=1, tiled=True)  16.8 us
    pallas_call x1, Pallas kernels, scan_stage(): pl.pallas_call(scan_kernel, name='scan', out_shape=(shape((STEPS, ROWS, C...  16.7 us
    pallas_call x1, Pallas kernels, step_stage(): pl.pallas_call(step_kernel, name='sizes', out_shape=(rows, rows, rows, ro...  9.16 us
  transfers between devices with their start and end apart: 21, of which 7 were waited for; matrix products, arithmetic and copies ran while one was open for 3% of the time, Pallas kernels for 9%

profile of v2, /device:TPU:40, one launch (start us, length us, event | category | flops | bytes accessed | tf_op | source)
XLA Modules:
  0.0 371.3 jit_solution(17524403785416274333)
XLA Ops:
  7.2 0.0 all-gather.6.cloned.1.call-start
  7.2 1.4 reshape.64.table_ref
  8.6 0.6 pad_add_fusion.me_ref
  9.2 106.6 %plan.1 = (s32[8,96]{1,0:T(8,128)}, s32[4,128]{1,0:T(4,128)}, s32[96,1]{1,0:T(8,128)}, s32[288,1]{1,0:T(8,128)}, s32[288,1]{1,0:T(8,128)}, /*index=5*/bf16[512,1...) custom-call(s32[4]{0:T(128)} %pad_add_fusion.me_ref, ...), custom_call_target="tpu_custom_call" | custom-call | tf_op jit(solution)/shard_map/plan/pallas_call | solution.py:131
  115.8 0.0 all-gather.6.cloned.1.call-update
  115.8 0.0 all-gather.4.cloned.1.call-start
  115.9 0.7 all-gather.4.cloned.1.call-update
  116.6 49.0 %all_to_all.10 = bf16[32,16,1024]{2,1,0:T(8,128)(2,1)} all-to-all(bf16[32,16,1024]{2,1,0:T(8,128)(2,1)} %bitcast.61), channel_id=1, replica_groups=mesh['z'=8,'x'=4,'y'=4,'c'=2] {'z','x'}, dimensions={0} | all-to-all | bytes 2097152 | tf_op jit(solution)/shard_map/all_to_all | solution.py:393
  165.6 6.2 %all-to-all-start = ((bf16[96,16,1024]{2,1,0:T(8,128)(2,1)}), bf16[96,16,1024]{2,1,0:T(8,128)(2,1)S(1)}, u32[]{:S(2)}, u32[]{:S(2)}) async-start(bf16[96,16,1024]{2,1,0:T(8,128)(2,1)} %get-tuple-element.24), calls=%async_computation | async-start | bytes 6291456 | tf_op jit(solution)/shard_map/all_to_all | solution.py:397
  171.8 0.0 reduce-scatter.2.cloned.1.call-start
  171.8 0.0 all-gather.6.cloned.1.call-done
  171.8 1.9 slice.24
  173.7 1.6 collective-permute-start.3
  175.3 2.5 collective-permute-start.4
  177.9 1.5 collective-permute-start.5
  179.3 36.3 %collective-permute-done.3.g1 = bf16[256,1024]{1,0:T(8,128)(2,1)} collective-permute-done((bf16[256,1024]{1,0:T(8,128)(2,1)}, bf16[256,1024]{1,0:T(8,128)(2,1)}, u32[]{:S(2)}, u32[]{:S(2)}) %collective-permute-start.3) | collective-permute-done | bytes 524320 | tf_op jit(solution)/shard_map/ppermute | solution.py:354
  215.6 7.1 %collective-permute-done.4.g2 = bf16[256,1024]{1,0:T(8,128)(2,1)} collective-permute-done((bf16[256,1024]{1,0:T(8,128)(2,1)}, bf16[256,1024]{1,0:T(8,128)(2,1)}, u32[]{:S(2)}, u32[]{:S(2)}) %collective-permute-start.4) | collective-permute-done | bytes 524320 | tf_op jit(solution)/shard_map/ppermute | solution.py:354
  222.7 4.0 %collective-permute-done.5.g3 = bf16[256,1024]{1,0:T(8,128)(2,1)} collective-permute-done((bf16[256,1024]{1,0:T(8,128)(2,1)}, bf16[256,1024]{1,0:T(8,128)(2,1)}, u32[]{:S(2)}, u32[]{:S(2)}) %collective-permute-start.5) | collective-permute-done | bytes 524320 | tf_op jit(solution)/shard_map/ppermute | solution.py:354
  226.7 7.7 %conv.1 = (f32[4,96,1024]{2,1,0:T(8,128)}, bf16[384,544]{1,0:T(8,128)(2,1)}, bf16[3,96,1024]{2,1,0:T(8,128)(2,1)}) custom-call(s32[4]{0:T(128)} %pad_add_fusion.me_ref, bf16[512,1024]{1,0:T(8,128)(2,1)} %bitcast.54, bf16[256,1024]{1,0:T(8,128)(2,1)} %bitcast.19.g0, bf16[256,1024]{1,0:T(8,128)(2,1)} %collective-permute-done.3.g1, ...), custom_call_target="tpu_custom_call" | custom-call | tf_op jit(solution)/shard_map/conv/pallas_call | solution.py:192
  234.4 1.0 dynamic-slice_bitcast_fusion
  235.4 0.1 collective-permute-start.6
  235.5 1.6 collective-permute-done.6
  237.1 1.1 convert_add_fusion
  238.2 0.8 copy-done.1
  239.1 0.7 dynamic-slice_bitcast_fusion.3
  239.8 0.1 collective-permute-start.9
  239.8 2.9 collective-permute-start.8
  242.7 1.9 collective-permute-start.7
  244.6 1.0 slice.25
  245.6 0.1 collective-permute-start.14
  245.7 3.0 collective-permute-start.15
  248.8 0.0 collective-permute-done.9
  248.8 0.0 collective-permute-done.8
  248.8 0.0 collective-permute-done.7
  248.8 1.0 fusion.2
  249.8 0.3 collective-permute-start.12
  250.1 3.1 collective-permute-start.11
  253.1 0.6 collective-permute-start.10
  253.7 0.6 fusion.3
  261.3 0.0 collective-permute-done.12
  261.3 2.0 collective-permute-start.16
  263.4 0.0 collective-permute-done.11
  263.4 0.0 collective-permute-done.10
  263.4 0.9 pad_maximum_fusion.own_ref
  264.3 0.1 collective-permute-start.13
  264.4 1.8 constant_dynamic-slice_fusion
  266.2 0.1 collective-permute-start
  266.3 2.0 collective-permute-start.1
  268.3 0.0 collective-permute-done.15.g2
  268.3 1.8 collective-permute-start.2
  270.1 6.9 %collective-permute-done.16.g3 = bf16[128,1024]{1,0:T(8,128)(2,1)S(1)} collective-permute-done((bf16[128,1024]{1,0:T(8,128)(2,1)S(1)}, bf16[128,1024]{1,0:T(8,128)(2,1)S(1)}, u32[]{:S(2)}, u32[]{:S(2)}) %collective-permute-start.16) | collective-permute-done | bytes 262176 | tf_op jit(solution)/shard_map/ppermute | solution.py:354
  277.0 0.7 copy-done.5
  277.7 0.0 copy-done.4
  277.7 9.2 %sizes.1 = (f32[4,96,1024]{2,1,0:T(8,128)}, f32[4,96,1024]{2,1,0:T(8,128)}, f32[4,96,1024]{2,1,0:T(8,128)}, f32[4,96,1024]{2,1,0:T(8,128)}, f32[4,32,96,128]{3,2,1,0:T(8,128)}, /*index=5*/f32[16,1024]{1,0:T(8,128)}) custom-call(s32[4]{0:T(128)} %pad_add_fusion.me_ref, bf16[4,48,544]{2,1,0:T(8,128)(2,1)} %copy-done.3, bf16[4,48,544]{2,1,0:T(8,128)(2,1)} %copy-done.5, ...), custom_call_target="tpu_custom_call" | custom-call | tf_op jit(solution)/shard_map/sizes/pallas_call | solution.py:246
  286.9 0.0 collective-permute-done
  286.9 0.0 collective-permute-done.1
  286.9 0.0 all-to-all-done.main_ref
  287.0 0.6 copy-done.6
  287.5 1.0 copy-done
  288.6 16.7 %scan.1 = (bf16[4,96,1024]{2,1,0:T(8,128)(2,1)}, bf16[96,16,1024]{2,1,0:T(8,128)(2,1)}) custom-call(s32[8,96]{1,0:T(8,128)} %get-tuple-element.23.at_ref, bf16[96,16,1024]{2,1,0:T(8,128)(2,1)} %copy-done, bf16[3,16,1024]{2,1,0:T(8,128)(2,1)} %bitcast.68, bf16[3,16,1024]{2,1,0:T(8,128)(2,1)} %bitcast.70, bf16[3,16,1024]{2,1,0:T(8,128)(2,1)} %bitcast.14.e2, ...), custom_call_target="tpu_custom_call" | custom-call | tf_op jit(solution)/shard_map/scan/pallas_call | solution.py:322
  305.3 16.8 %all-gather.4.cloned.1.call-done = bf16[1024,4096]{1,0:T(8,128)(2,1)} async-done(((bf16[1024,128]{1,0:T(8,128)(2,1)}), bf16[1024,4096]{1,0:T(8,128)(2,1)}) %all-gather.4.cloned.1.call-update) | async-done | bytes 8388624 | tf_op jit(solution)/shard_map/all_gather | solution.py:396
  322.2 8.7 %convolution_convert_fusion = bf16[384,4096]{1,0:T(8,128)(2,1)} fusion(bf16[384,1024]{1,0:T(8,128)(2,1)} %bitcast.78, bf16[1024,4096]{1,0:T(8,128)(2,1)} %all-gather.4.cloned.1.call-done), kind=kOutput, calls=%fused_computation | convolution fusion | flops 3222798336 | bytes 12320768 | tf_op jit(solution)/shard_map/dot_general | solution.py:39
  330.8 0.0 reduce-scatter.2.cloned.1.call-update
  330.9 33.9 %reduce-scatter.2.cloned.1.call-done = bf16[384,512]{1,0:T(8,128)(2,1)} async-done(((bf16[384,4096]{1,0:T(8,128)(2,1)}), bf16[384,512]{1,0:T(8,128)(2,1)}) %reduce-scatter.2.cloned.1.call-update) | async-done | bytes 393232 | tf_op jit(solution)/shard_map/reduce_scatter | solution.py:418
  (15 shorter events, 0.1 us)
Async XLA Ops:
  7.2 164.7 %all-gather.6.cloned.1.call-start = ((), (), s32[]{:S(2)}) async-start(), calls=%async_computation.5 | async-start | bytes 1769472 | tf_op jit(solution)/shard_map/all_gather | solution.py:392
  115.8 206.3 %all-gather.4.cloned.1.call-start = ((), (), s32[]{:S(2)}) async-start(), calls=%async_computation.3 | async-start | bytes 8650752 | tf_op jit(solution)/shard_map/all_gather | solution.py:396
  165.6 121.4 %all-to-all-start = ((bf16[96,16,1024]{2,1,0:T(8,128)(2,1)}), bf16[96,16,1024]{2,1,0:T(8,128)(2,1)S(1)}, u32[]{:S(2)}, u32[]{:S(2)}) async-start(bf16[96,16,1024]{2,1,0:T(8,128)(2,1)} %get-tuple-element.24), calls=%async_computation | async-start | bytes 6291456 | tf_op jit(solution)/shard_map/all_to_all | solution.py:397
  171.8 193.0 %reduce-scatter.2.cloned.1.call-start = ((), (), s32[]{:S(2)}) async-start(), calls=%async_computation.4 | async-start | bytes 3538944 | tf_op jit(solution)/shard_map/reduce_scatter | solution.py:418
  173.7 41.9 %collective-permute-start.3 = (bf16[256,1024]{1,0:T(8,128)(2,1)}, bf16[256,1024]{1,0:T(8,128)(2,1)}, u32[]{:S(2)}, u32[]{:S(2)}) collective-permute-start(bf16[256,1024]{1,0:T(8,128)(2,1)} %bitcast.19.g0), channel_id=1, source_target_pairs={{0,8},{8,16},{16,24},{24,0},{1,9},{9,17},{17,25},{25,1},{2,10},{10... | collective-permute-start | bytes 1572872 | tf_op jit(solution)/shard_map/ppermute | solution.py:354
  175.3 47.4 %collective-permute-start.4 = (bf16[256,1024]{1,0:T(8,128)(2,1)}, bf16[256,1024]{1,0:T(8,128)(2,1)}, u32[]{:S(2)}, u32[]{:S(2)}) collective-permute-start(bf16[256,1024]{1,0:T(8,128)(2,1)} %bitcast.19.g0), channel_id=1, source_target_pairs={{0,16},{8,24},{16,0},{24,8},{1,17},{9,25},{17,1},{25,9},{2,18},{10... | collective-permute-start | bytes 1572872 | tf_op jit(solution)/shard_map/ppermute | solution.py:354
  177.9 48.9 %collective-permute-start.5 = (bf16[256,1024]{1,0:T(8,128)(2,1)}, bf16[256,1024]{1,0:T(8,128)(2,1)}, u32[]{:S(2)}, u32[]{:S(2)}) collective-permute-start(bf16[256,1024]{1,0:T(8,128)(2,1)} %bitcast.19.g0), channel_id=1, source_target_pairs={{0,24},{8,0},{16,8},{24,16},{1,25},{9,1},{17,9},{25,17},{2,26},{10... | collective-permute-start | bytes 1572872 | tf_op jit(solution)/shard_map/ppermute | solution.py:354
  226.7 27.0 %copy-start.7 = (s32[4,128]{1,0:T(4,128)S(1)}, s32[4,128]{1,0:T(4,128)}, u32[]{:S(2)}) copy-start(s32[4,128]{1,0:T(4,128)} %get-tuple-element.26) | copy-start | bytes 6148
  235.4 1.7 collective-permute-start.6
  238.2 0.8 copy-start.1
  239.8 9.0 %collective-permute-start.9 = (bf16[48,544]{1,0:T(8,128)(2,1)}, bf16[48,544]{1,0:T(8,128)(2,1)S(1)}, u32[]{:S(2)}, u32[]{:S(2)}) collective-permute-start(bf16[48,544]{1,0:T(8,128)(2,1)} %get-tuple-element.48), channel_id=1, source_target_pairs={{0,6},{2,0},{4,2},{6,4},{1,7},{3,1},{5,3},{7,5},{8,14},{10,8},{12,... | collective-permute-start | bytes 156680 | tf_op jit(solution)/shard_map/ppermute | solution.py:354
  239.8 8.9 %collective-permute-start.8 = (bf16[48,544]{1,0:T(8,128)(2,1)}, bf16[48,544]{1,0:T(8,128)(2,1)}, u32[]{:S(2)}, u32[]{:S(2)}) collective-permute-start(bf16[48,544]{1,0:T(8,128)(2,1)} %get-tuple-element.49), channel_id=1, source_target_pairs={{0,4},{2,6},{4,0},{6,2},{1,5},{3,7},{5,1},{7,3},{8,12},{10,14},{12... | collective-permute-start | bytes 156680 | tf_op jit(solution)/shard_map/ppermute | solution.py:354
  242.7 6.0 %collective-permute-start.7 = (bf16[48,544]{1,0:T(8,128)(2,1)S(1)}, bf16[48,544]{1,0:T(8,128)(2,1)}, u32[]{:S(2)}, u32[]{:S(2)}) collective-permute-start(bf16[48,544]{1,0:T(8,128)(2,1)S(1)} %get-tuple-element.47), channel_id=1, source_target_pairs={{0,2},{2,4},{4,6},{6,0},{1,3},{3,5},{5,7},{7,1},{8,10},{10,12},{12... | collective-permute-start | bytes 156680 | tf_op jit(solution)/shard_map/ppermute | solution.py:354
  245.6 32.1 %copy-start.2 = (bf16[8,16,1024]{2,1,0:T(8,128)(2,1)}, bf16[8,16,1024]{2,1,0:T(8,128)(2,1)S(1)}, u32[]{:S(2)}) copy-start(bf16[8,16,1024]{2,1,0:T(8,128)(2,1)S(1)} %slice.25) | copy-start | bytes 786436
  245.6 20.7 %collective-permute-start.14 = (bf16[128,1024]{1,0:T(8,128)(2,1)S(1)}, bf16[128,1024]{1,0:T(8,128)(2,1)}, u32[]{:S(2)}, u32[]{:S(2)}) collective-permute-start(bf16[128,1024]{1,0:T(8,128)(2,1)S(1)} %bitcast.57), channel_id=1, source_target_pairs={{0,8},{8,16},{16,24},{24,0},{1,9},{9,17},{17,25},{25,1},{2,10},{10... | collective-permute-start | bytes 786440 | tf_op jit(solution)/shard_map/ppermute | solution.py:354
  245.7 22.6 %collective-permute-start.15 = (bf16[128,1024]{1,0:T(8,128)(2,1)S(1)}, bf16[128,1024]{1,0:T(8,128)(2,1)}, u32[]{:S(2)}, u32[]{:S(2)}) collective-permute-start(bf16[128,1024]{1,0:T(8,128)(2,1)S(1)} %bitcast.58), channel_id=1, source_target_pairs={{0,16},{8,24},{16,0},{24,8},{1,17},{9,25},{17,1},{25,9},{2,18},{10... | collective-permute-start | bytes 786440 | tf_op jit(solution)/shard_map/ppermute | solution.py:354
  249.8 11.5 %collective-permute-start.12 = (bf16[48,544]{1,0:T(8,128)(2,1)S(1)}, bf16[48,544]{1,0:T(8,128)(2,1)S(1)}, u32[]{:S(2)}, u32[]{:S(2)}) collective-permute-start(bf16[48,544]{1,0:T(8,128)(2,1)S(1)} %fusion.2), channel_id=1, source_target_pairs={{0,2},{2,4},{4,6},{6,0},{1,3},{3,5},{5,7},{7,1},{8,10},{10,12},{12... | collective-permute-start | bytes 156680 | tf_op jit(solution)/shard_map/ppermute | solution.py:354
  250.1 13.3 %collective-permute-start.11 = (bf16[48,544]{1,0:T(8,128)(2,1)S(1)}, bf16[48,544]{1,0:T(8,128)(2,1)}, u32[]{:S(2)}, u32[]{:S(2)}) collective-permute-start(bf16[48,544]{1,0:T(8,128)(2,1)S(1)} %fusion.2), channel_id=1, source_target_pairs={{0,4},{2,6},{4,0},{6,2},{1,5},{3,7},{5,1},{7,3},{8,12},{10,14},{12... | collective-permute-start | bytes 156680 | tf_op jit(solution)/shard_map/ppermute | solution.py:354
  253.1 10.2 %collective-permute-start.10 = (bf16[48,544]{1,0:T(8,128)(2,1)S(1)}, bf16[48,544]{1,0:T(8,128)(2,1)}, u32[]{:S(2)}, u32[]{:S(2)}) collective-permute-start(bf16[48,544]{1,0:T(8,128)(2,1)S(1)} %fusion.2), channel_id=1, source_target_pairs={{0,6},{2,0},{4,2},{6,4},{1,7},{3,1},{5,3},{7,5},{8,14},{10,8},{12,... | collective-permute-start | bytes 156680 | tf_op jit(solution)/shard_map/ppermute | solution.py:354
  261.3 15.7 %collective-permute-start.16 = (bf16[128,1024]{1,0:T(8,128)(2,1)S(1)}, bf16[128,1024]{1,0:T(8,128)(2,1)S(1)}, u32[]{:S(2)}, u32[]{:S(2)}) collective-permute-start(bf16[128,1024]{1,0:T(8,128)(2,1)S(1)} %bitcast.59), channel_id=1, source_target_pairs={{0,24},{8,0},{16,8},{24,16},{1,25},{9,1},{17,9},{25,17},{2,26},{10... | collective-permute-start | bytes 786440 | tf_op jit(solution)/shard_map/ppermute | solution.py:354
  264.3 13.4 %copy-start.3 = (bf16[4,48,544]{2,1,0:T(8,128)(2,1)}, bf16[4,48,544]{2,1,0:T(8,128)(2,1)S(1)}, u32[]{:S(2)}) copy-start(bf16[4,48,544]{2,1,0:T(8,128)(2,1)S(1)} %pad_maximum_fusion.own_ref) | copy-start | bytes 626692
  264.3 12.7 %collective-permute-start.13 = (bf16[4,48,544]{2,1,0:T(8,128)(2,1)S(1)}, bf16[4,48,544]{2,1,0:T(8,128)(2,1)S(1)}, u32[]{:S(2)}, u32[]{:S(2)}) collective-permute-start(bf16[4,48,544]{2,1,0:T(8,128)(2,1)S(1)} %pad_maximum_fusion.own_ref), channel_id=1, source_target_pairs={{0,1},{1,0},{2,3},{3,2},{4,5},{5,4},{6,7},{7,6},{8,9},{9,8},{10,11... | collective-permute-start | bytes 626696 | tf_op jit(solution)/shard_map/ppermute | solution.py:354
  266.2 20.7 %collective-permute-start = (bf16[1,48,1024]{2,1,0:T(8,128)(2,1)}, bf16[1,48,1024]{2,1,0:T(8,128)(2,1)S(1)}, u32[]{:S(2)}, u32[]{:S(2)}) collective-permute-start(bf16[1,48,1024]{2,1,0:T(8,128)(2,1)} %get-tuple-element.45), channel_id=1, source_target_pairs={{0,8},{8,16},{16,24},{24,0},{1,9},{9,17},{17,25},{25,1},{2,10},{10... | collective-permute-start | bytes 294920 | tf_op jit(solution)/shard_map/ppermute | solution.py:354
  266.3 20.6 %collective-permute-start.1 = (bf16[1,48,1024]{2,1,0:T(8,128)(2,1)}, bf16[1,48,1024]{2,1,0:T(8,128)(2,1)}, u32[]{:S(2)}, u32[]{:S(2)}) collective-permute-start(bf16[1,48,1024]{2,1,0:T(8,128)(2,1)} %get-tuple-element.44), channel_id=1, source_target_pairs={{0,16},{8,24},{16,0},{24,8},{1,17},{9,25},{17,1},{25,9},{2,18},{10... | collective-permute-start | bytes 294920 | tf_op jit(solution)/shard_map/ppermute | solution.py:354
  268.3 18.6 %collective-permute-start.2 = (bf16[1,48,1024]{2,1,0:T(8,128)(2,1)}, bf16[1,48,1024]{2,1,0:T(8,128)(2,1)}, u32[]{:S(2)}, u32[]{:S(2)}) collective-permute-start(bf16[1,48,1024]{2,1,0:T(8,128)(2,1)} %get-tuple-element.43), channel_id=1, source_target_pairs={{0,24},{8,0},{16,8},{24,16},{1,25},{9,1},{17,9},{25,17},{2,26},{10... | collective-permute-start | bytes 294920 | tf_op jit(solution)/shard_map/ppermute | solution.py:354
  277.0 0.8 copy-start.4
  277.0 0.7 copy-start.5
  286.9 0.6 copy-start.6
  286.9 1.6 copy-start
Sparse Core Ops, SparseCore 0:
  116.0 55.7 all-gather.5
  174.8 147.3 all-gather.3
  331.0 33.7 reduce-scatter.1

commit v3 on v2

--- a/solution.py
+++ b/solution.py
@@ -22,9 +22,8 @@
 COEF = LOW // GROUPS
 DELTA = RANK // GROUPS
 BASE = ROWS // GROUPS
-SLOT = 16
-SEC = 32
-GATH = SEC + DELTA
+SLOT = 24
+GATH = 40
 LOG2E = 1.4426950408889634
 VMEM = pl.BlockSpec(memory_space=pltpu.VMEM)
 SMEM = pl.BlockSpec(memory_space=pltpu.SMEM)
@@ -48,14 +47,13 @@
 
 
 def plan_kernel(
-    me_ref, slots_ref, remaining_ref, table_ref, conv_ref, coef_ref, delta_ref, ssm_ref, proj_ref,
-    gather_ref, relay_ref, rem_ref, col_ref, ext_ref, buf_ref, block_ref, main_ref, proj_out_ref,
+    me_ref, slots_ref, remaining_ref, table_ref, conv_ref, ssm_ref,
+    gather_ref, relay_ref, rem_ref, col_ref, buf_ref, extra_ref, main_ref,
     pick_ref, pick_smem, sems,
 ):
     me = me_ref[0]
     x = me_ref[1]
-    passed = pltpu.make_async_copy(proj_ref, proj_out_ref, sems.at[3])
-    passed.start()
+    z = me // NX
     square = (ROWS, ROWS)
     eye = iota(square, 0) == iota(square, 1)
     to_row = table_ref[pl.ds(me, 1), :] // ROWS
@@ -72,7 +70,7 @@
     picking.wait()
     for p in range(BASE):
         pltpu.make_async_copy(
-            ssm_ref.at[pick_smem[0, ROWS + p]], block_ref.at[pl.ds(GATH + p * STATE, STATE)], sems.at[2]
+            ssm_ref.at[pick_smem[0, ROWS + p]], extra_ref.at[pl.ds(p * STATE, STATE)], sems.at[2]
         ).start()
 
     def send(p, carry):
@@ -81,15 +79,10 @@
 
     lax.fori_loop(0, ROWS, send, 0)
     buf = jnp.zeros((GROUPS * SLOT, CH), F32)
-    sec = bdot(onehot(iota((SEC, COEF), 0) == iota((SEC, COEF), 1)), coef_ref[...])
     for tap in range(3):
-        dest = jnp.where(order_row < BASE, to_row * SLOT + order_row * 3 + tap, -1)
+        dest = to_row * SLOT + order_row * 3 + tap
         buf += bdot(onehot(iota((GROUPS * SLOT, ROWS), 0) == dest), conv_ref[tap])
-        dest = jnp.where(order_row < BASE, -1, COEF + (order_row - BASE) * 3 + tap)
-        sec += bdot(onehot(iota((SEC, ROWS), 0) == dest), conv_ref[tap])
     buf_ref[...] = buf.astype(BF)
-    block_ref[pl.ds(0, SEC), :] = sec.astype(BF)
-    block_ref[pl.ds(SEC, DELTA), :] = delta_ref[...]
     match = (slots_ref[...] == me * ROWS + iota((ROWS, GROUPS * ROWS), 0)).astype(I32)
     inv = jnp.sum(match * iota(match.shape, 1), axis=1, keepdims=True)
     rem_ref[...] = jnp.sum(match * remaining_ref[...], axis=1, keepdims=True)
@@ -102,73 +95,65 @@
     rank_row = jnp.sum(
         ((src == src_row) & (inv < inv_row)).astype(I32), axis=0, keepdims=True
     )
-    turn = lax.rem(x - lax.rem(src_row, NX) + NX, NX)
+    turn = lax.rem(z - src_row // NX + NZ, NZ)
     where_row = jnp.where(rank_row < BASE, src_row * BASE + rank_row, ROWS + (turn - 1) * BASE + rank_row)
     gather_ref[...] = jnp.broadcast_to(where_row, gather_ref.shape)
     for tap in range(3):
-        at = pl.ds(tap * ROWS, ROWS)
-        col_ref[at, :] = jnp.where(rank < BASE, src * SLOT + rank * 3 + tap, -1)
-        ext_ref[at, :] = jnp.where(
-            rank < BASE, -1, src * SEC + COEF + (rank - BASE) * 3 + tap
-        )
+        col_ref[pl.ds(tap * ROWS, ROWS), :] = src * SLOT + rank * 3 + tap
     target = table_ref[...] // ROWS
     groups = iota((GROUPS, 1), 0)
-    for k in range(NX):
-        dest = me - x + lax.rem(x + k, NX)
+    for k in range(NZ):
+        dest = lax.rem(z + k, NZ) * NX + x
         count = jnp.sum((target == dest).astype(I32), axis=1, keepdims=True)
-        holds = (count > BASE) & (lax.rem(groups, NX) == x)
-        z = jnp.sum(jnp.where(holds, groups // NX, 0), axis=0, keepdims=True)
-        relay_ref[pl.ds(k, 1), :] = jnp.broadcast_to(z, (1, 128))
+        holds = (count > BASE) & (groups // NX == z)
+        spot = jnp.sum(jnp.where(holds, lax.rem(x - lax.rem(groups, NX) + NX, NX), 0), axis=0, keepdims=True)
+        relay_ref[pl.ds(k, 1), :] = jnp.broadcast_to(spot, (1, 128))
     pltpu.make_async_copy(
-        ssm_ref.at[pl.ds(0, BASE)].reshape(BASE * STATE, CH), block_ref.at[pl.ds(GATH, BASE * STATE)], sems.at[2]
+        ssm_ref.at[pl.ds(0, BASE)].reshape(BASE * STATE, CH), extra_ref, sems.at[2]
     ).wait()
     pltpu.make_async_copy(ssm_ref, main_ref, sems.at[1]).wait()
-    passed.wait()
-
-
-def plan(me, slots, remaining, table, conv, coef, delta, ssm, proj):
+
+
+def plan(me, slots, remaining, table, conv, ssm):
     shape = jax.ShapeDtypeStruct
     return pl.pallas_call(
         plan_kernel,
         name="plan",
         out_shape=(
             shape((8, ROWS), I32),
-            shape((NX, 128), I32),
+            shape((NZ, 128), I32),
             shape((ROWS, 1), I32),
             shape((3 * ROWS, 1), I32),
-            shape((3 * ROWS, 1), I32),
             shape((GROUPS * SLOT, CH), BF),
-            shape((GATH + BASE * STATE, CH), BF),
+            shape((BASE * STATE, CH), BF),
             shape((ROWS, STATE, CH), BF),
-            shape(proj.shape, BF),
-        ),
-        in_specs=[SMEM] + [VMEM] * 6 + [ANY] * 2,
-        out_specs=(VMEM,) * 7 + (ANY,) * 2,
+        ),
+        in_specs=[SMEM] + [VMEM] * 4 + [ANY],
+        out_specs=(VMEM,) * 7,
         scratch_shapes=[
             pltpu.VMEM((8, 128), I32),
             pltpu.SMEM((8, 128), I32),
-            pltpu.SemaphoreType.DMA((4,)),
+            pltpu.SemaphoreType.DMA((3,)),
         ],
+        cost_estimate=pl.CostEstimate(flops=1 << 33, bytes_accessed=12 << 20, transcendentals=0),
         compiler_params=pltpu.CompilerParams(vmem_limit_bytes=60 << 20),
-    )(me, slots, remaining, table, conv, coef, delta, ssm, proj)
+    )(me, slots, remaining, table, conv, ssm)
 
 
 def conv_kernel(
-    me_ref, moved_ref, g0, g1, g2, g3, col_ref, ext_ref, rem_ref, inputs_ref, weight_ref, bias_ref,
+    me_ref, moved_ref, g0, g1, g2, g3, col_ref, rem_ref, inputs_ref, weight_ref, bias_ref,
     act_ref, low_ref, final_ref,
 ):
     x = me_ref[1]
     parts = (g0, g1, g2, g3)
-    span = NZ * SEC
+    span = NZ * GATH
     window = bdot(onehot(col_ref[...] == iota((3 * ROWS, GROUPS * SLOT), 1)), moved_ref[...])
     coef = jnp.zeros((LOW, CH), F32)
     for k, part in enumerate(parts):
         at = iota((1, span), 1)
-        z, q = at // SEC, at % SEC
+        z, q = at // GATH, at % GATH
         group = z * NX + lax.rem(x - k + NX, NX)
-        ext = onehot(ext_ref[...] == group * SEC + q)
-        window += bdot(ext, part[...])
-        row = jnp.where(q < COEF, group * COEF + q, -1)
+        row = jnp.where((q >= DELTA) & (q < DELTA + COEF), group * COEF + q - DELTA, -1)
         coef += bdot(onehot(iota((LOW, span), 0) == row), part[...])
     coef = coef.astype(BF)
     taps = [window[tap * ROWS : (tap + 1) * ROWS] for tap in range(3)]
@@ -187,7 +172,7 @@
         final_ref[k] = kept.astype(BF)
 
 
-def conv_stage(me, moved, parts, col, ext, rem, inputs, weight, bias):
+def conv_stage(me, moved, parts, col, rem, inputs, weight, bias):
     shape = jax.ShapeDtypeStruct
     return pl.pallas_call(
         conv_kernel,
@@ -197,10 +182,10 @@
             shape((STEPS * ROWS, LOW), BF),
             shape((3, ROWS, CH), BF),
         ),
-        in_specs=[SMEM] + [VMEM] * 11,
+        in_specs=[SMEM] + [VMEM] * 10,
         out_specs=(VMEM,) * 3,
         compiler_params=pltpu.CompilerParams(vmem_limit_bytes=60 << 20),
-    )(me, moved, *parts, col, ext, rem, inputs, weight, bias)
+    )(me, moved, *parts, col, rem, inputs, weight, bias)
 
 
 def step_kernel(
@@ -214,12 +199,13 @@
         for m in range(NY):
             at = half * NY + lax.rem(y + m, NY)
             low_ref[pl.ds(pl.multiple_of(at * chunk, 16), chunk), :] = piece[m]
-    span = NZ * DELTA
+    span = NZ * GATH
     delta = jnp.zeros((RANK, CH), F32)
     for k, part in enumerate((g0, g1, g2, g3)):
         at = iota((1, span), 1)
-        z, q = at // DELTA, at % DELTA
-        row = (z * NX + lax.rem(x - k + NX, NX)) * DELTA + q
+        z, q = at // GATH, at % GATH
+        group = z * NX + lax.rem(x - k + NX, NX)
+        row = jnp.where(q < DELTA, group * DELTA + q, -1)
         delta += bdot(onehot(iota((RANK, span), 0) == row), part[...])
     delta = delta.astype(BF)
     rem = rem_ref[...]
@@ -259,7 +245,7 @@
 
 
 def scan_kernel(
-    at_ref, main_ref, e0, e1, e2, e3, dt_ref, dx_ref, sk_ref, sg_ref, bc_ref, rate_ref,
+    at_ref, main_ref, extra_ref, dt_ref, dx_ref, sk_ref, sg_ref, bc_ref, rate_ref,
     out_ref, final_ref, held, wide, sems,
 ):
     b = pl.program_id(0)
@@ -272,12 +258,10 @@
             def _():
                 pltpu.make_async_copy(main_ref.at[at], held.at[block, i], sems.at[block]).start()
 
-            for k, extra in enumerate((e0, e1, e2, e3)):
-                row = at - ROWS - k * BASE
-
-                @pl.when((row >= 0) & (row < BASE))
-                def _(row=row, extra=extra):
-                    pltpu.make_async_copy(extra.at[row], held.at[block, i], sems.at[block]).start()
+            @pl.when(at >= ROWS)
+            def _():
+                rows = pl.ds(pl.multiple_of((at - ROWS) * STATE, STATE), STATE)
+                pltpu.make_async_copy(extra_ref.at[rows], held.at[block, i], sems.at[block]).start()
 
     @pl.when(b == 0)
     def _():
@@ -316,7 +300,7 @@
             final_ref[i, :, pl.ds(l * 128, 128)] = wide[l, pl.ds(i * STATE, STATE), :].astype(BF)
 
 
-def scan_stage(at, main, extras, dt, dx, sk, sg, bc, rate):
+def scan_stage(at, main, extra, dt, dx, sk, sg, bc, rate):
     shape = jax.ShapeDtypeStruct
     rows = pl.BlockSpec((STEPS, BLOCK, CH), lambda b, at: (0, b, 0))
     return pl.pallas_call(
@@ -327,9 +311,6 @@
             num_scalar_prefetch=1,
             grid=(BLOCKS,),
             in_specs=[
-                ANY,
-                ANY,
-                ANY,
                 ANY,
                 ANY,
                 rows,
@@ -347,7 +328,78 @@
             ],
         ),
         compiler_params=pltpu.CompilerParams(vmem_limit_bytes=60 << 20),
-    )(at, main, *extras, dt, dx, sk, sg, bc, rate)
+    )(at, main, extra, dt, dx, sk, sg, bc, rate)
+
+
+def after_kernel(*refs):
+    pass
+
+
+def after(value, *others):
+    return pl.pallas_call(
+        after_kernel,
+        name="after",
+        out_shape=jax.ShapeDtypeStruct(value.shape, value.dtype),
+        in_specs=[ANY] * (1 + len(others)),
+        out_specs=ANY,
+        input_output_aliases={0: 0},
+    )(value, *others)
+
+
+def theirs_kernel(me_ref, rows_ref, proj_ref, out_ref):
+    out_ref[0] = bdot(rows_ref[...], proj_ref[...]).astype(BF)
+
+
+def ours_kernel(me_ref, rows_ref, proj_ref, got_ref, out_ref):
+    out_ref[0] = (bdot(rows_ref[...], proj_ref[...]) + got_ref[0].astype(F32)).astype(BF)
+
+
+def mix(me, rows, proj):
+    shape = jax.ShapeDtypeStruct
+    count, width = rows.shape[0], proj.shape[1] // (NY * NC)
+    params = pltpu.CompilerParams(vmem_limit_bytes=60 << 20)
+    whole = pl.BlockSpec((count, CH), lambda i, me: (0, 0))
+    sums = shape((NY, count, width), BF)
+
+    def block(index):
+        return pl.BlockSpec((1, count, width), lambda i, me: (index(i, me), 0, 0))
+
+    def columns(index):
+        return pl.BlockSpec((CH, width), lambda i, me: (0, index(i, me)))
+
+    given = pl.pallas_call(
+        theirs_kernel,
+        name="theirs",
+        out_shape=sums,
+        grid_spec=pltpu.PrefetchScalarGridSpec(
+            num_scalar_prefetch=1,
+            grid=(NY,),
+            in_specs=[whole, columns(lambda i, me: i * NC + 1 - me[3])],
+            out_specs=block(lambda i, me: i),
+        ),
+        compiler_params=params,
+    )(me, rows, proj)
+    got = shift(given, "c", NC, 1)
+    parts = pl.pallas_call(
+        ours_kernel,
+        name="ours",
+        out_shape=sums,
+        grid_spec=pltpu.PrefetchScalarGridSpec(
+            num_scalar_prefetch=1,
+            grid=(NY,),
+            in_specs=[
+                whole,
+                columns(lambda i, me: lax.rem(me[2] + i, NY) * NC + me[3]),
+                block(lambda i, me: lax.rem(me[2] + i, NY)),
+            ],
+            out_specs=block(lambda i, me: i),
+        ),
+        compiler_params=params,
+    )(me, rows, proj, got)
+    total = parts[0].astype(F32)
+    for s in range(1, NY):
+        total += shift(parts[s], "y", NY, s).astype(F32)
+    return total.astype(BF)
 
 
 def shift(value, axis, size, k):
@@ -378,45 +430,40 @@
     z, x, y, c = (lax.axis_index(name) for name in ("z", "x", "y", "c"))
     group = z * NX + x
     me = jnp.stack([group, x, y, c]).astype(I32)
-    at, relay, rem, col, ext, buf, block, main, proj = plan(
+    proj = lax.all_gather(out_proj, ("z", "x"), axis=1, tiled=True)
+
+    def exchange(value, axes):
+        return lax.all_to_all(value, axes, split_axis=0, concat_axis=0, tiled=True)
+
+    def turned(value):
+        return [value] + [shift(value, "x", NX, k) for k in range(1, NX)]
+
+    first = jnp.concatenate([delta_proj, coef_proj.T, jnp.zeros((GATH - COEF - DELTA, CH), BF)], axis=0)
+    gathered = exchange(jnp.broadcast_to(first[None], (NZ, GATH, CH)), "z")
+    parts = turned(gathered.reshape(NZ * GATH, CH))
+    at, relay, rem, col, buf, extra, main = plan(
         me,
         new_slot.reshape(1, -1),
         remaining.reshape(1, -1),
         new_slot.reshape(GROUPS, ROWS),
         conv_state.transpose(1, 0, 2),
-        coef_proj.T,
-        delta_proj,
         ssm_state,
-        out_proj,
-    )
-    gathered = lax.all_gather(block, "z", axis=0)
-    moved = lax.all_to_all(
-        buf.reshape(GROUPS, SLOT, CH), ("z", "x"), split_axis=0, concat_axis=0, tiled=True
-    ).reshape(GROUPS * SLOT, CH)
-    out_whole = lax.all_gather(proj, ("z", "x"), axis=1, tiled=True)
-    ssm_main = lax.all_to_all(main, ("z", "x"), split_axis=0, concat_axis=0, tiled=True)
-
-    def turned(value):
-        return [value] + [shift(value, "x", NX, k) for k in range(1, NX)]
-
-    secs = turned(gathered[:, :SEC].reshape(NZ * SEC, CH))
-    deltas = turned(gathered[:, SEC:GATH].reshape(NZ * DELTA, CH))
-    extras = [
-        lax.dynamic_slice(gathered, (relay[k, 0], GATH, 0), (1, BASE * STATE, CH)) for k in range(NX)
-    ]
-    extras = [extras[0]] + [shift(extras[k], "x", NX, k) for k in range(1, NX)]
-    extras = [e.reshape(BASE, STATE, CH) for e in extras]
+    )
+    moved = exchange(after(buf, gathered).reshape(GROUPS, SLOT, CH), ("z", "x")).reshape(GROUPS * SLOT, CH)
+    ssm_main = exchange(after(main, moved, *parts[1:]), ("z", "x"))
+    beside = jnp.stack(turned(extra))
+    extras = [lax.dynamic_index_in_dim(beside, relay[k, 0], 0, False) for k in range(NZ)]
+    extras = [extras[0]] + [shift(extras[k], "z", NZ, k) for k in range(1, NZ)]
     act, low, conv_final = conv_stage(
-        me, moved, secs, col, ext, rem, input_steps, conv_weight, conv_bias.reshape(1, -1)
+        me, moved, parts, col, rem, input_steps, conv_weight, conv_bias.reshape(1, -1)
     )
     own, other = reduce_mp(low, y, c)
-    dt, dx, sk, sg, bc, rate = step_stage(
-        me, own, other, deltas, delta_bias.reshape(1, -1), act, gate_steps, skip_gain.reshape(1, -1), rem, decay_log
-    )
-    stepped, ssm_final = scan_stage(at, ssm_main, extras, dt, dx, sk, sg, bc, rate)
-    partial_mix = bdot(stepped.reshape(STEPS * ROWS, CH), out_whole)
-    summed = lax.psum_scatter(partial_mix.astype(BF), ("y", "c"), scatter_dimension=1, tiled=True)
-    return summed.reshape(STEPS, ROWS, -1), conv_final.transpose(1, 0, 2), ssm_final
+    sized = step_stage(
+        me, own, other, parts, delta_bias.reshape(1, -1), act, gate_steps, skip_gain.reshape(1, -1), rem, decay_log
+    )
+    stepped, ssm_final = scan_stage(at, ssm_main, jnp.concatenate(extras, axis=0), *sized)
+    mixed = mix(me, stepped.reshape(STEPS * ROWS, CH), proj)
+    return mixed.reshape(STEPS, ROWS, -1), conv_final.transpose(1, 0, 2), ssm_final
 
 
 def solution(mesh):

time: 376 us -> 327 us (0.87)
  Pallas kernels: 140 us -> 54.4 us
  blocking collectives: 49 us -> 0 us
  waiting for transfers between devices: 107 us -> 150 us
  starting transfers between devices: 29.9 us -> 65.7 us
  matrix products: 8.69 us -> 0 us
  between operations: 21 us -> 29.1 us
  local copies, waits for them, and re-layouts: 11.5 us -> 16.4 us
    pallas_call x1, Pallas kernels: 107 us -> 6.43 us  [plan(): pl.pallas_call(plan_kernel, name='plan', out_shape=(shape((8, ROWS), I32)...]
    ppermute x17 -> x25, waiting for transfers between devices: 55.9 us -> 137 us  [shift(): return lax.ppermute(value, axis, [(i, (i + k) % size) for i in range(size)])]
    all_to_all x1 -> x0, blocking collectives: 49 us -> none  [per_device(): lax.all_to_all(buf.reshape(GROUPS, SLOT, CH), ('z', 'x'), split_axis=0, c...]
    reduce_scatter x1 -> x0, waiting for transfers between devices: 33.9 us -> none  [per_device(): lax.psum_scatter(partial_mix.astype(BF), ('y', 'c'), scatter_dimension=1,...]
    all_to_all x1 -> x3, starting transfers between devices: 6.18 us -> 24.3 us  [exchange(): return lax.all_to_all(value, axes, split_axis=0, concat_axis=0, tiled=True)]
    ppermute x17 -> x25, starting transfers between devices: 23.6 us -> 41.4 us  [shift(): return lax.ppermute(value, axis, [(i, (i + k) % size) for i in range(size)])]
    all_gather x2 -> x1, waiting for transfers between devices: 16.8 us -> 0.02 us  [per_device(): proj = lax.all_gather(out_proj, ('z', 'x'), axis=1, tiled=True)]
    all_to_all x1 -> x3, waiting for transfers between devices: 0.01 us -> 12.6 us  [exchange(): return lax.all_to_all(value, axes, split_axis=0, concat_axis=0, tiled=True)]
  transfers between devices with their start and end apart: 21 -> 29, of which waited for: 7 -> 13; matrix products, arithmetic and copies ran while one was open for 3% -> 4% of each run, Pallas kernels for 9% -> 13%
where the time goes in v3:
time: 327 us; the launch traced here: 321 us
  waiting for transfers between devices  150 us (46%)
  starting transfers between devices  65.7 us (20%)
  Pallas kernels  54.4 us (17%)
  between operations  29.1 us (9%)
  local copies, waits for them, and re-layouts  16.4 us (5%)
  other arithmetic  4.62 us (1%)
    ppermute x25, waiting for transfers between devices, shift(): return lax.ppermute(value, axis, [(i, (i + k) % size) for i in range(size)])  137 us
    ppermute x25, starting transfers between devices, shift(): return lax.ppermute(value, axis, [(i, (i + k) % size) for i in range(size)])  41.4 us
    all_to_all x3, starting transfers between devices, exchange(): return lax.all_to_all(value, axes, split_axis=0, concat_axis=0, tiled=True)  24.3 us
    pallas_call x1, Pallas kernels, scan_stage(): pl.pallas_call(scan_kernel, name='scan', out_shape=(shape((STEPS, ROWS, C...  16.6 us
    all_to_all x3, waiting for transfers between devices, exchange(): return lax.all_to_all(value, axes, split_axis=0, concat_axis=0, tiled=True)  12.6 us
    unnamed x33, local copies, waits for them, and re-layouts  10.9 us
    pallas_call x1, Pallas kernels, step_stage(): pl.pallas_call(step_kernel, name='sizes', out_shape=(rows, rows, rows, ro...  10.6 us
    pallas_call x1, Pallas kernels, conv_stage(): pl.pallas_call(conv_kernel, name='conv', out_shape=(shape((STEPS, ROWS, C...  8.31 us
  transfers between devices with their start and end apart: 29, of which 13 were waited for; matrix products, arithmetic and copies ran while one was open for 4% of the time, Pallas kernels for 13%

profile of v3, /device:TPU:40, one launch (start us, length us, event | category | flops | bytes accessed | tf_op | source)
XLA Modules:
  0.0 320.7 jit_solution(4441665100527560331)
XLA Ops:
  7.2 0.7 all-gather.2.cloned.1.call-update
  8.0 0.9 maximum_maximum_fusion
  8.9 0.9 broadcast_in_dim.10
  9.8 8.6 %all-to-all-start = ((bf16[8,40,1024]{2,1,0:T(8,128)(2,1)}), bf16[8,40,1024]{2,1,0:T(8,128)(2,1)S(1)}, u32[]{:S(2)}, u32[]{:S(2)}) async-start(bf16[8,40,1024]{2,1,0:T(8,128)(2,1)} %broadcast_in_dim.10), calls=%async_computation | async-start | bytes 1310720 | tf_op jit(solution)/shard_map/all_to_all | solution.py:436
  18.4 0.7 reshape.52.table_ref
  19.1 0.6 pad_add_fusion.me_ref
  19.7 6.4 %plan.1 = (s32[8,96]{1,0:T(8,128)}, s32[8,128]{1,0:T(8,128)}, s32[96,1]{1,0:T(8,128)}, s32[288,1]{1,0:T(8,128)}, bf16[768,1024]{1,0:T(8,128)(2,1)}, /*index=5*/b...) custom-call(s32[4]{0:T(128)} %pad_add_fusion.me_ref, s32[1,3072]{1,0:T(1,128)} %bitcast.105, s32[1,3072]{1,0:T(1,128)} %bitcast.111, ...), custom_call_target="tpu_custom_call" | custom-call | flops 8589934592 | bytes 12582912 | tf_op jit(solution)/shard_map/plan/pallas_call | solution.py:119
  26.1 12.6 %all-to-all-done.refs_1_ = bf16[8,40,1024]{2,1,0:T(8,128)(2,1)S(1)} async-done(((bf16[8,40,1024]{2,1,0:T(8,128)(2,1)}), bf16[8,40,1024]{2,1,0:T(8,128)(2,1)S(1)}, u32[]{:S(2)}, u32[]{:S(2)}) %all-to-all-start) | async-done | bytes 655392 | tf_op jit(solution)/shard_map/all_to_all | solution.py:436
  38.7 0.9 copy-done.2
  39.6 7.1 %all-to-all-start.1 = ((bf16[32,24,1024]{2,1,0:T(8,128)(2,1)}), bf16[32,24,1024]{2,1,0:T(8,128)(2,1)S(1)}, u32[]{:S(2)}, u32[]{:S(2)}) async-start(bf16[32,24,1024]{2,1,0:T(8,128)(2,1)} %bitcast.88), calls=%async_computation.1 | async-start | bytes 3145728 | tf_op jit(solution)/shard_map/all_to_all | solution.py:436
  46.7 1.5 collective-permute-start
  48.3 2.7 collective-permute-start.1
  50.9 1.5 collective-permute-start.2
  52.4 22.3 %collective-permute-done.refs_2_.g1 = bf16[320,1024]{1,0:T(8,128)(2,1)S(1)} collective-permute-done((bf16[320,1024]{1,0:T(8,128)(2,1)S(1)}, bf16[320,1024]{1,0:T(8,128)(2,1)S(1)}, u32[]{:S(2)}, u32[]{:S(2)}) %collective-permute-start) | collective-permute-done | bytes 655392 | tf_op jit(solution)/shard_map/ppermute | solution.py:406
  74.7 26.7 %collective-permute-done.1.refs_3_.g2 = bf16[320,1024]{1,0:T(8,128)(2,1)S(1)} collective-permute-done((bf16[320,1024]{1,0:T(8,128)(2,1)S(1)}, bf16[320,1024]{1,0:T(8,128)(2,1)S(1)}, u32[]{:S(2)}, u32[]{:S(2)}) %collective-permute-start.1) | collective-permute-done | bytes 655392 | tf_op jit(solution)/shard_map/ppermute | solution.py:406
  101.4 0.9 copy-done.5
  102.3 1.1 copy-done
  103.4 8.6 %all-to-all-start.2 = ((bf16[96,16,1024]{2,1,0:T(8,128)(2,1)}), bf16[96,16,1024]{2,1,0:T(8,128)(2,1)S(1)}, u32[]{:S(2)}, u32[]{:S(2)}) async-start(bf16[96,16,1024]{2,1,0:T(8,128)(2,1)} %after.3), calls=%async_computation.2 | async-start | bytes 6291456 | tf_op jit(solution)/shard_map/all_to_all | solution.py:436
  112.0 2.8 collective-permute-start.5
  114.7 0.9 collective-permute-start.4
  115.6 0.9 collective-permute-start.3
  116.5 0.6 fusion.6
  131.9 4.9 %collective-permute-done.5 = bf16[48,1024]{1,0:T(8,128)(2,1)S(1)} collective-permute-done((bf16[48,1024]{1,0:T(8,128)(2,1)S(1)}, bf16[48,1024]{1,0:T(8,128)(2,1)S(1)}, u32[]{:S(2)}, u32[]{:S(2)}) %collective-permute-start.5) | collective-permute-done | bytes 98336 | tf_op jit(solution)/shard_map/ppermute | solution.py:406
  136.8 0.8 dynamic-slice_bitcast_fusion.1
  137.7 1.7 collective-permute-start.6
  139.4 5.2 %collective-permute-start.7 = (bf16[48,1024]{1,0:T(8,128)(2,1)}, bf16[48,1024]{1,0:T(8,128)(2,1)}, u32[]{:S(2)}, u32[]{:S(2)}) collective-permute-start(bf16[48,1024]{1,0:T(8,128)(2,1)} %get-tuple-element.47), channel_id=1, source_target_pairs={{0,64},{32,96},{64,128},{96,160},{128,192},{160,224},{192,0},{224,... | collective-permute-start | bytes 294920 | tf_op jit(solution)/shard_map/ppermute | solution.py:406
  144.6 0.9 collective-permute-start.8
  145.5 0.9 collective-permute-start.9
  146.4 3.6 %collective-permute-start.10 = (bf16[48,1024]{1,0:T(8,128)(2,1)}, bf16[48,1024]{1,0:T(8,128)(2,1)}, u32[]{:S(2)}, u32[]{:S(2)}) collective-permute-start(bf16[48,1024]{1,0:T(8,128)(2,1)} %get-tuple-element.44), channel_id=1, source_target_pairs={{0,160},{32,192},{64,224},{96,0},{128,32},{160,64},{192,96},{224,1... | collective-permute-start | bytes 294920 | tf_op jit(solution)/shard_map/ppermute | solution.py:406
  150.0 59.0 %collective-permute-done.6 = bf16[48,1024]{1,0:T(8,128)(2,1)S(1)} collective-permute-done((bf16[48,1024]{1,0:T(8,128)(2,1)S(1)}, bf16[48,1024]{1,0:T(8,128)(2,1)S(1)}, u32[]{:S(2)}, u32[]{:S(2)}) %collective-permute-start.6) | collective-permute-done | bytes 98336 | tf_op jit(solution)/shard_map/ppermute | solution.py:406
  208.9 2.7 collective-permute-start.11
  211.6 8.3 %conv.1 = (f32[4,96,1024]{2,1,0:T(8,128)}, bf16[384,544]{1,0:T(8,128)(2,1)}, bf16[3,96,1024]{2,1,0:T(8,128)(2,1)}) custom-call(s32[4]{0:T(128)} %pad_add_fusion.me_ref, bf16[768,1024]{1,0:T(8,128)(2,1)} %bitcast.82, bf16[320,1024]{1,0:T(8,128)(2,1)} %bitcast.83, bf16[320,1024]{1,0:T(8,128)(2,1)} %copy-done.4, bf16[320,1024]{1,0:T(8,128)(2,1)} %copy-done.5, ...), custom_call_target="tpu_custom_call" | custom-call | tf_op jit(solution)/shard_map/conv/pallas_call | solution.py:177
  219.9 1.0 dynamic-slice_bitcast_fusion
  221.0 0.9 constant_dynamic-update-slice_fusion.5
  221.9 0.9 constant_dynamic-update-slice_fusion.4
  222.8 1.0 convert_add_fusion.1
  224.4 2.0 collective-permute-start.15
  226.4 2.0 collective-permute-start.14
  228.4 0.9 constant_dynamic-update-slice_fusion.3
  229.3 1.2 collective-permute-start.12
  230.5 1.0 collective-permute-done.14
  231.5 1.5 collective-permute-start.19
  233.1 3.0 collective-permute-start.18
  236.1 0.6 collective-permute-start.17
  236.6 0.9 constant_dynamic-update-slice_fusion.2
  237.5 1.4 collective-permute-done.18
  238.9 1.4 collective-permute-done.17
  240.7 0.9 constant_dynamic-update-slice_fusion.1
  242.2 0.7 copy-done.9
  242.9 10.6 %sizes.1 = (f32[4,96,1024]{2,1,0:T(8,128)}, f32[4,96,1024]{2,1,0:T(8,128)}, f32[4,96,1024]{2,1,0:T(8,128)}, f32[4,96,1024]{2,1,0:T(8,128)}, f32[4,32,96,128]{3,2,1,0:T(8,128)}, /*index=5*/f32[16,1024]{1,0:T(8,128)}) custom-call(s32[4]{0:T(128)} %pad_add_fusion.me_ref, bf16[4,48,544]{2,1,0:T(8,128)(2,1)} %copy-done.8, bf16[4,48,544]{2,1,0:T(8,128)(2,1)} %copy-done.9, ...), custom_call_target="tpu_custom_call" | custom-call | tf_op jit(solution)/shard_map/sizes/pallas_call | solution.py:232
  253.4 1.6 copy-done.1
  255.1 16.6 %scan.1 = (bf16[4,96,1024]{2,1,0:T(8,128)(2,1)}, bf16[96,16,1024]{2,1,0:T(8,128)(2,1)}) custom-call(s32[8,96]{1,0:T(8,128)} %get-tuple-element.21.at_ref, bf16[96,16,1024]{2,1,0:T(8,128)(2,1)} %copy-done.1, bf16[384,1024]{1,0:T(8,128)(2,1)} %copy-done.7, f32[4,96,1024]{2,1,0:T(8,128)} %get-tuple-element.30.dt_ref, f32[4,96,1024]{2,1,0:T(8,128)} %get-tuple-element.31.dx_ref, ...), custom_call_target="tpu_custom_call" | custom-call | tf_op jit(solution)/shard_map/scan/pallas_call | solution.py:306
  271.7 6.1 %theirs.1 = bf16[4,384,512]{2,1,0:T(8,128)(2,1)} custom-call(s32[4]{0:T(128)} %pad_add_fusion.me_ref, bf16[384,1024]{1,0:T(8,128)(2,1)} %bitcast.89, bf16[1024,4096]{1,0:T(8,128)(2,1)} %all-gather.2.cloned.1.call-done.proj_ref), custom_call_target="tpu_custom_call" | custom-call | tf_op jit(solution)/shard_map/theirs/pallas_call | solution.py:370
  278.1 3.3 %collective-permute-done.21.got_ref = bf16[4,384,512]{2,1,0:T(8,128)(2,1)S(1)} collective-permute-done((bf16[4,384,512]{2,1,0:T(8,128)(2,1)}, bf16[4,384,512]{2,1,0:T(8,128)(2,1)S(1)}, u32[]{:S(2)}, u32[]{:S(2)}) %collective-permute-start.21) | collective-permute-done | bytes 1572896 | tf_op jit(solution)/shard_map/ppermute | solution.py:406
  281.5 1.1 copy-done.6
  282.6 6.3 %ours.1 = bf16[4,384,512]{2,1,0:T(8,128)(2,1)} custom-call(s32[4]{0:T(128)} %pad_add_fusion.me_ref, bf16[384,1024]{1,0:T(8,128)(2,1)} %bitcast.90, bf16[1024,4096]{1,0:T(8,128)(2,1)} %all-gather.2.cloned.1.call-done.proj_ref, bf16[4,384,512]{2,1,0:T(8,128)(2,1)} %copy-done.6), custom_call_target="tpu_custom_call" | custom-call | tf_op jit(solution)/shard_map/ours/pallas_call | solution.py:383
  289.0 1.3 slice_bitcast_fusion.2
  290.3 0.7 collective-permute-start.24
  291.0 1.6 collective-permute-start.23
  292.6 2.5 collective-permute-start.22
  295.2 6.5 %collective-permute-done.24 = bf16[384,512]{1,0:T(8,128)(2,1)S(1)} collective-permute-done((bf16[384,512]{1,0:T(8,128)(2,1)S(1)}, bf16[384,512]{1,0:T(8,128)(2,1)S(1)}, u32[]{:S(2)}, u32[]{:S(2)}) %collective-permute-start.24) | collective-permute-done | bytes 393248 | tf_op jit(solution)/shard_map/ppermute | solution.py:406
  301.7 8.8 %collective-permute-done.23 = bf16[384,512]{1,0:T(8,128)(2,1)S(1)} collective-permute-done((bf16[384,512]{1,0:T(8,128)(2,1)S(1)}, bf16[384,512]{1,0:T(8,128)(2,1)S(1)}, u32[]{:S(2)}, u32[]{:S(2)}) %collective-permute-start.23) | collective-permute-done | bytes 393248 | tf_op jit(solution)/shard_map/ppermute | solution.py:406
  310.5 1.4 collective-permute-done.22
  311.9 1.9 fusion.2
  (54 shorter events, 2.2 us)
Async XLA Ops:
  7.2 11.2 %copy-start.11 = (s32[3072]{0:T(1024)S(1)}, s32[3072]{0:T(1024)}, u32[]{:S(2)}) copy-start(s32[3072]{0:T(1024)} %param.18) | copy-start | bytes 36868
  7.2 264.5 %all-gather.2.cloned.1.call-start = ((), (), s32[]{:S(2)}) async-start(), calls=%async_computation.3 | async-start | bytes 8650752 | tf_op jit(solution)/shard_map/all_gather | solution.py:433
  9.8 28.9 %all-to-all-start = ((bf16[8,40,1024]{2,1,0:T(8,128)(2,1)}), bf16[8,40,1024]{2,1,0:T(8,128)(2,1)S(1)}, u32[]{:S(2)}, u32[]{:S(2)}) async-start(bf16[8,40,1024]{2,1,0:T(8,128)(2,1)} %broadcast_in_dim.10), calls=%async_computation | async-start | bytes 1310720 | tf_op jit(solution)/shard_map/all_to_all | solution.py:436
  38.7 0.9 copy-start.2
  39.6 7.2 %copy-start.3 = (bf16[8,40,1024]{2,1,0:T(8,128)(2,1)S(1)}, bf16[8,40,1024]{2,1,0:T(8,128)(2,1)}, u32[]{:S(2)}) copy-start(bf16[8,40,1024]{2,1,0:T(8,128)(2,1)} %copy-done.2) | copy-start | bytes 1966084
  39.6 62.7 %all-to-all-start.1 = ((bf16[32,24,1024]{2,1,0:T(8,128)(2,1)}), bf16[32,24,1024]{2,1,0:T(8,128)(2,1)S(1)}, u32[]{:S(2)}, u32[]{:S(2)}) async-start(bf16[32,24,1024]{2,1,0:T(8,128)(2,1)} %bitcast.88), calls=%async_computation.1 | async-start | bytes 3145728 | tf_op jit(solution)/shard_map/all_to_all | solution.py:436
  46.7 27.9 %collective-permute-start = (bf16[320,1024]{1,0:T(8,128)(2,1)S(1)}, bf16[320,1024]{1,0:T(8,128)(2,1)S(1)}, u32[]{:S(2)}, u32[]{:S(2)}) collective-permute-start(bf16[320,1024]{1,0:T(8,128)(2,1)S(1)} %bitcast.85), channel_id=1, source_target_pairs={{0,8},{8,16},{16,24},{24,0},{1,9},{9,17},{17,25},{25,1},{2,10},{10... | collective-permute-start | bytes 1966088 | tf_op jit(solution)/shard_map/ppermute | solution.py:406
  48.3 53.1 %collective-permute-start.1 = (bf16[320,1024]{1,0:T(8,128)(2,1)S(1)}, bf16[320,1024]{1,0:T(8,128)(2,1)S(1)}, u32[]{:S(2)}, u32[]{:S(2)}) collective-permute-start(bf16[320,1024]{1,0:T(8,128)(2,1)S(1)} %bitcast.86), channel_id=1, source_target_pairs={{0,16},{8,24},{16,0},{24,8},{1,17},{9,25},{17,1},{25,9},{2,18},{10... | collective-permute-start | bytes 1966088 | tf_op jit(solution)/shard_map/ppermute | solution.py:406
  50.9 51.3 %collective-permute-start.2 = (bf16[320,1024]{1,0:T(8,128)(2,1)S(1)}, bf16[320,1024]{1,0:T(8,128)(2,1)}, u32[]{:S(2)}, u32[]{:S(2)}) collective-permute-start(bf16[320,1024]{1,0:T(8,128)(2,1)S(1)} %bitcast.87), channel_id=1, source_target_pairs={{0,24},{8,0},{16,8},{24,16},{1,25},{9,1},{17,9},{25,17},{2,26},{10... | collective-permute-start | bytes 1966088 | tf_op jit(solution)/shard_map/ppermute | solution.py:406
  74.7 27.6 %copy-start.4 = (bf16[320,1024]{1,0:T(8,128)(2,1)}, bf16[320,1024]{1,0:T(8,128)(2,1)S(1)}, u32[]{:S(2)}) copy-start(bf16[320,1024]{1,0:T(8,128)(2,1)S(1)} %collective-permute-done.refs_2_.g1) | copy-start | bytes 1966084
  101.4 0.9 copy-start.5
  102.3 1.1 copy-start
  103.4 8.6 %copy-start.10 = (bf16[48,1024]{1,0:T(8,128)(2,1)S(1)}, bf16[48,1024]{1,0:T(8,128)(2,1)}, u32[]{:S(2)}) copy-start(bf16[48,1024]{1,0:T(8,128)(2,1)} %get-tuple-element.24) | copy-start | bytes 294916
  103.4 13.1 %copy-start.12 = (s32[8,128]{1,0:T(8,128)S(1)}, s32[8,128]{1,0:T(8,128)}, u32[]{:S(2)}) copy-start(s32[8,128]{1,0:T(8,128)} %get-tuple-element.25) | copy-start | bytes 12292
  103.4 150.0 %all-to-all-start.2 = ((bf16[96,16,1024]{2,1,0:T(8,128)(2,1)}), bf16[96,16,1024]{2,1,0:T(8,128)(2,1)S(1)}, u32[]{:S(2)}, u32[]{:S(2)}) async-start(bf16[96,16,1024]{2,1,0:T(8,128)(2,1)} %after.3), calls=%async_computation.2 | async-start | bytes 6291456 | tf_op jit(solution)/shard_map/all_to_all | solution.py:436
  112.0 24.8 %collective-permute-start.5 = (bf16[48,1024]{1,0:T(8,128)(2,1)S(1)}, bf16[48,1024]{1,0:T(8,128)(2,1)S(1)}, u32[]{:S(2)}, u32[]{:S(2)}) collective-permute-start(bf16[48,1024]{1,0:T(8,128)(2,1)S(1)} %copy-done.10), channel_id=1, source_target_pairs={{0,24},{8,0},{16,8},{24,16},{1,25},{9,1},{17,9},{25,17},{2,26},{10... | collective-permute-start | bytes 294920 | tf_op jit(solution)/shard_map/ppermute | solution.py:406
  114.7 22.0 %collective-permute-start.4 = (bf16[48,1024]{1,0:T(8,128)(2,1)S(1)}, bf16[48,1024]{1,0:T(8,128)(2,1)S(1)}, u32[]{:S(2)}, u32[]{:S(2)}) collective-permute-start(bf16[48,1024]{1,0:T(8,128)(2,1)S(1)} %copy-done.10), channel_id=1, source_target_pairs={{0,16},{8,24},{16,0},{24,8},{1,17},{9,25},{17,1},{25,9},{2,18},{10... | collective-permute-start | bytes 294920 | tf_op jit(solution)/shard_map/ppermute | solution.py:406
  115.6 21.2 %collective-permute-start.3 = (bf16[48,1024]{1,0:T(8,128)(2,1)S(1)}, bf16[48,1024]{1,0:T(8,128)(2,1)S(1)}, u32[]{:S(2)}, u32[]{:S(2)}) collective-permute-start(bf16[48,1024]{1,0:T(8,128)(2,1)S(1)} %copy-done.10), channel_id=1, source_target_pairs={{0,8},{8,16},{16,24},{24,0},{1,9},{9,17},{17,25},{25,1},{2,10},{10... | collective-permute-start | bytes 294920 | tf_op jit(solution)/shard_map/ppermute | solution.py:406
  137.7 71.3 %collective-permute-start.6 = (bf16[48,1024]{1,0:T(8,128)(2,1)S(1)}, bf16[48,1024]{1,0:T(8,128)(2,1)S(1)}, u32[]{:S(2)}, u32[]{:S(2)}) collective-permute-start(bf16[48,1024]{1,0:T(8,128)(2,1)S(1)} %get-tuple-element.48), channel_id=1, source_target_pairs={{0,32},{32,64},{64,96},{96,128},{128,160},{160,192},{192,224},{224... | collective-permute-start | bytes 294920 | tf_op jit(solution)/shard_map/ppermute | solution.py:406
  139.4 81.5 %collective-permute-start.7 = (bf16[48,1024]{1,0:T(8,128)(2,1)}, bf16[48,1024]{1,0:T(8,128)(2,1)}, u32[]{:S(2)}, u32[]{:S(2)}) collective-permute-start(bf16[48,1024]{1,0:T(8,128)(2,1)} %get-tuple-element.47), channel_id=1, source_target_pairs={{0,64},{32,96},{64,128},{96,160},{128,192},{160,224},{192,0},{224,... | collective-permute-start | bytes 294920 | tf_op jit(solution)/shard_map/ppermute | solution.py:406
  144.6 77.4 %collective-permute-start.8 = (bf16[48,1024]{1,0:T(8,128)(2,1)}, bf16[48,1024]{1,0:T(8,128)(2,1)}, u32[]{:S(2)}, u32[]{:S(2)}) collective-permute-start(bf16[48,1024]{1,0:T(8,128)(2,1)} %get-tuple-element.46), channel_id=1, source_target_pairs={{0,96},{32,128},{64,160},{96,192},{128,224},{160,0},{192,32},{224,... | collective-permute-start | bytes 294920 | tf_op jit(solution)/shard_map/ppermute | solution.py:406
  145.5 81.0 %collective-permute-start.9 = (bf16[48,1024]{1,0:T(8,128)(2,1)}, bf16[48,1024]{1,0:T(8,128)(2,1)}, u32[]{:S(2)}, u32[]{:S(2)}) collective-permute-start(bf16[48,1024]{1,0:T(8,128)(2,1)} %get-tuple-element.45), channel_id=1, source_target_pairs={{0,128},{32,160},{64,192},{96,224},{128,0},{160,32},{192,64},{224,... | collective-permute-start | bytes 294920 | tf_op jit(solution)/shard_map/ppermute | solution.py:406
  146.4 89.7 %collective-permute-start.10 = (bf16[48,1024]{1,0:T(8,128)(2,1)}, bf16[48,1024]{1,0:T(8,128)(2,1)}, u32[]{:S(2)}, u32[]{:S(2)}) collective-permute-start(bf16[48,1024]{1,0:T(8,128)(2,1)} %get-tuple-element.44), channel_id=1, source_target_pairs={{0,160},{32,192},{64,224},{96,0},{128,32},{160,64},{192,96},{224,1... | collective-permute-start | bytes 294920 | tf_op jit(solution)/shard_map/ppermute | solution.py:406
  208.9 31.7 %collective-permute-start.11 = (bf16[48,1024]{1,0:T(8,128)(2,1)S(1)}, bf16[48,1024]{1,0:T(8,128)(2,1)}, u32[]{:S(2)}, u32[]{:S(2)}) collective-permute-start(bf16[48,1024]{1,0:T(8,128)(2,1)S(1)} %get-tuple-element.43), channel_id=1, source_target_pairs={{0,192},{32,224},{64,0},{96,32},{128,64},{160,96},{192,128},{224,1... | collective-permute-start | bytes 294920 | tf_op jit(solution)/shard_map/ppermute | solution.py:406
  220.9 1.9 collective-permute-start.13
  223.9 5.4 %collective-permute-start.16 = (bf16[48,544]{1,0:T(8,128)(2,1)S(1)}, bf16[48,544]{1,0:T(8,128)(2,1)S(1)}, u32[]{:S(2)}, u32[]{:S(2)}) collective-permute-start(bf16[48,544]{1,0:T(8,128)(2,1)S(1)} %get-tuple-element.50), channel_id=1, source_target_pairs={{0,6},{2,0},{4,2},{6,4},{1,7},{3,1},{5,3},{7,5},{8,14},{10,8},{12,... | collective-permute-start | bytes 156680 | tf_op jit(solution)/shard_map/ppermute | solution.py:406
  224.4 6.1 %collective-permute-start.15 = (bf16[48,544]{1,0:T(8,128)(2,1)S(1)}, bf16[48,544]{1,0:T(8,128)(2,1)S(1)}, u32[]{:S(2)}, u32[]{:S(2)}) collective-permute-start(bf16[48,544]{1,0:T(8,128)(2,1)S(1)} %get-tuple-element.51), channel_id=1, source_target_pairs={{0,4},{2,6},{4,0},{6,2},{1,5},{3,7},{5,1},{7,3},{8,12},{10,14},{12... | collective-permute-start | bytes 156680 | tf_op jit(solution)/shard_map/ppermute | solution.py:406
  226.4 5.1 %collective-permute-start.14 = (bf16[48,544]{1,0:T(8,128)(2,1)S(1)}, bf16[48,544]{1,0:T(8,128)(2,1)S(1)}, u32[]{:S(2)}, u32[]{:S(2)}) collective-permute-start(bf16[48,544]{1,0:T(8,128)(2,1)S(1)} %get-tuple-element.49), channel_id=1, source_target_pairs={{0,2},{2,4},{4,6},{6,0},{1,3},{3,5},{5,7},{7,1},{8,10},{10,12},{12... | collective-permute-start | bytes 156680 | tf_op jit(solution)/shard_map/ppermute | solution.py:406
  229.3 12.3 %collective-permute-start.12 = (bf16[48,1024]{1,0:T(8,128)(2,1)S(1)}, bf16[48,1024]{1,0:T(8,128)(2,1)S(1)}, u32[]{:S(2)}, u32[]{:S(2)}) collective-permute-start(bf16[48,1024]{1,0:T(8,128)(2,1)S(1)} %get-tuple-element.42), channel_id=1, source_target_pairs={{0,224},{32,0},{64,32},{96,64},{128,96},{160,128},{192,160},{224,1... | collective-permute-start | bytes 294920 | tf_op jit(solution)/shard_map/ppermute | solution.py:406
  231.5 6.0 %collective-permute-start.19 = (bf16[48,544]{1,0:T(8,128)(2,1)S(1)}, bf16[48,544]{1,0:T(8,128)(2,1)S(1)}, u32[]{:S(2)}, u32[]{:S(2)}) collective-permute-start(bf16[48,544]{1,0:T(8,128)(2,1)S(1)} %fusion.5), channel_id=1, source_target_pairs={{0,2},{2,4},{4,6},{6,0},{1,3},{3,5},{5,7},{7,1},{8,10},{10,12},{12... | collective-permute-start | bytes 156680 | tf_op jit(solution)/shard_map/ppermute | solution.py:406
  233.1 5.8 %collective-permute-start.18 = (bf16[48,544]{1,0:T(8,128)(2,1)S(1)}, bf16[48,544]{1,0:T(8,128)(2,1)S(1)}, u32[]{:S(2)}, u32[]{:S(2)}) collective-permute-start(bf16[48,544]{1,0:T(8,128)(2,1)S(1)} %fusion.5), channel_id=1, source_target_pairs={{0,4},{2,6},{4,0},{6,2},{1,5},{3,7},{5,1},{7,3},{8,12},{10,14},{12... | collective-permute-start | bytes 156680 | tf_op jit(solution)/shard_map/ppermute | solution.py:406
  236.1 4.2 %collective-permute-start.17 = (bf16[48,544]{1,0:T(8,128)(2,1)S(1)}, bf16[48,544]{1,0:T(8,128)(2,1)S(1)}, u32[]{:S(2)}, u32[]{:S(2)}) collective-permute-start(bf16[48,544]{1,0:T(8,128)(2,1)S(1)} %fusion.5), channel_id=1, source_target_pairs={{0,6},{2,0},{4,2},{6,4},{1,7},{3,1},{5,3},{7,5},{8,14},{10,8},{12,... | collective-permute-start | bytes 156680 | tf_op jit(solution)/shard_map/ppermute | solution.py:406
  240.3 1.3 copy-start.8
  240.3 1.8 collective-permute-start.20
  241.6 1.2 copy-start.7
  242.2 0.7 copy-start.9
  253.4 1.6 copy-start.1
  277.8 3.6 %collective-permute-start.21 = (bf16[4,384,512]{2,1,0:T(8,128)(2,1)}, bf16[4,384,512]{2,1,0:T(8,128)(2,1)S(1)}, u32[]{:S(2)}, u32[]{:S(2)}) collective-permute-start(bf16[4,384,512]{2,1,0:T(8,128)(2,1)} %theirs.1), channel_id=1, source_target_pairs={{0,1},{1,0},{2,3},{3,2},{4,5},{5,4},{6,7},{7,6},{8,9},{9,8},{10,11... | collective-permute-start | bytes 4718600 | tf_op jit(solution)/shard_map/ppermute | solution.py:406
  281.5 1.1 copy-start.6
  290.3 11.4 %collective-permute-start.24 = (bf16[384,512]{1,0:T(8,128)(2,1)S(1)}, bf16[384,512]{1,0:T(8,128)(2,1)S(1)}, u32[]{:S(2)}, u32[]{:S(2)}) collective-permute-start(bf16[384,512]{1,0:T(8,128)(2,1)S(1)} %get-tuple-element.40), channel_id=1, source_target_pairs={{0,6},{2,0},{4,2},{6,4},{1,7},{3,1},{5,3},{7,5},{8,14},{10,8},{12,... | collective-permute-start | bytes 1179656 | tf_op jit(solution)/shard_map/ppermute | solution.py:406
  291.0 19.5 %collective-permute-start.23 = (bf16[384,512]{1,0:T(8,128)(2,1)S(1)}, bf16[384,512]{1,0:T(8,128)(2,1)S(1)}, u32[]{:S(2)}, u32[]{:S(2)}) collective-permute-start(bf16[384,512]{1,0:T(8,128)(2,1)S(1)} %get-tuple-element.41), channel_id=1, source_target_pairs={{0,4},{2,6},{4,0},{6,2},{1,5},{3,7},{5,1},{7,3},{8,12},{10,14},{12... | collective-permute-start | bytes 1179656 | tf_op jit(solution)/shard_map/ppermute | solution.py:406
  292.6 19.3 %collective-permute-start.22 = (bf16[384,512]{1,0:T(8,128)(2,1)S(1)}, bf16[384,512]{1,0:T(8,128)(2,1)S(1)}, u32[]{:S(2)}, u32[]{:S(2)}) collective-permute-start(bf16[384,512]{1,0:T(8,128)(2,1)S(1)} %get-tuple-element.39), channel_id=1, source_target_pairs={{0,2},{2,4},{4,6},{6,0},{1,3},{3,5},{5,7},{7,1},{8,10},{10,12},{12... | collective-permute-start | bytes 1179656 | tf_op jit(solution)/shard_map/ppermute | solution.py:406
Sparse Core Ops, SparseCore 0:
  10.5 208.1 all-gather.1
